TPU v7x, 512 devices: a whole 4x4x16 slice. The times are simulated.
512 devices in a mesh: dom: 16 (over z), feat: 32 (over x, y, core).
Axes of the slice: x: 4, y: 4, z: 16, core: 2. Of those that a mesh axis runs over, the one named last changes fastest.
Arguments:
- node_feats: bfloat16 [1024, 65536], P('feat', 'dom'), may hold values from -6 to 6
- out_cotangent: bfloat16 [1024, 65536], P('feat', 'dom'), may hold values from -6 to 6
- weight_self: bfloat16 [1024, 1024], P('feat'), may hold values from -0.1875 to 0.1875
- weight_neigh: bfloat16 [1024, 1024], P('feat'), may hold values from -1.5 to 1.5
- out_bias: float32 [1024], P('feat'), may hold values from -3 to 3
- send_blocks: int32 [16, 16, 2], P('dom'), may hold values from 0 to 31
- tile_rows: int32 [16, 64], P('dom'), may hold values from 0 to 31
- tile_cols: int32 [16, 64], P('dom'), may hold values from 0 to 63
- tile_count: int32 [16], P('dom'), may hold values from 1 to 64, as said below
- tile_values: bfloat16 [16, 64, 128, 128], P('dom'), may hold values from 0 to 1
Outputs:
- layer_out: bfloat16 [1024, 65536], P('feat', 'dom')
- feats_grad: bfloat16 [1024, 65536], P('feat', 'dom')
- grad_self: float32 [1024, 1024], P('feat')
- grad_neigh: float32 [1024, 1024], P('feat')
- grad_bias: float32 [1024], P('feat')
Inputs may be any that keep to these rules, and one draw needn't show every extreme that they name: Slots t >= tile_count[p] of tile_rows, tile_cols and tile_values are not part of the graph; some partition uses all 64 slots.
All inputs are finite; a program needn't handle non-finite values.
Results may differ from a plain program's by a relative error of at most 0.0075.
Values may be sent and summed in bfloat16 or wider, within the bound.
No kernel may reach another device: no remote copies, remote signals or barrier semaphores. Data moves between devices by JAX's collectives and lax.ppermute only.
A program may use at most 64 MiB of HBM per device.

v0:
```python
import jax
import jax.numpy as jnp
from jax import lax
from jax.sharding import PartitionSpec as P

BLK = 128
NBLK = 32
CAP = 2
TMAX = 64
ROWS = 4096


def gelu_tanh(values):
    return jax.nn.gelu(values, approximate=True)


def left_product(weights, data):
    return lax.dot_general(
        weights, data, (((0,), (0,)), ((), ())), preferred_element_type=jnp.float32
    )


def per_device(
    node_feats,
    out_cotangent,
    weight_self,
    weight_neigh,
    out_bias,
    send_blocks,
    tile_rows,
    tile_cols,
    tile_count,
    tile_values,
):
    highest = lax.Precision.HIGHEST
    local_width = node_feats.shape[0]
    num_parts = lax.axis_size("dom")
    ext_blocks = NBLK + num_parts * CAP
    my_sends = send_blocks[0].reshape(num_parts * CAP)
    my_rows = tile_rows[0]
    my_cols = tile_cols[0]
    my_tiles = tile_values[0]
    live = (jnp.arange(TMAX, dtype=jnp.int32) < tile_count[0]).astype(jnp.float32)
    blocks = node_feats.reshape(local_width, NBLK, BLK)
    outgoing = blocks[:, my_sends].reshape(local_width, num_parts * CAP * BLK)
    incoming = lax.all_to_all(outgoing, "dom", split_axis=1, concat_axis=1, tiled=True)
    extended = jnp.concatenate(
        [blocks, incoming.reshape(local_width, num_parts * CAP, BLK)], axis=1
    )
    rows_hot = jax.nn.one_hot(my_rows, NBLK, dtype=jnp.float32) * live[:, None]
    picked = extended[:, my_cols]
    products = jnp.einsum("ftc,trc->ftr", picked, my_tiles, preferred_element_type=jnp.float32)
    summed = jnp.einsum("ftr,tb->fbr", products, rows_hot, precision=highest)
    degree = jnp.einsum(
        "tr,tb->br", jnp.sum(my_tiles, axis=-1, dtype=jnp.float32), rows_hot, precision=highest
    )
    divisor = jnp.maximum(degree, 1.0)
    aggregate = (summed / divisor[None]).astype(jnp.bfloat16).reshape(local_width, ROWS)
    feat_rows, agg_rows = (
        lax.all_to_all(node_feats, "feat", split_axis=1, concat_axis=0, tiled=True),
        lax.all_to_all(aggregate, "feat", split_axis=1, concat_axis=0, tiled=True),
    )
    totals = left_product(lax.all_gather(weight_self, "feat", axis=0, tiled=True), feat_rows)
    out_by_rows = totals + left_product(
        lax.all_gather(weight_neigh, "feat", axis=0, tiled=True), agg_rows
    )
    pre_act = lax.all_to_all(out_by_rows, "feat", split_axis=0, concat_axis=1, tiled=True)
    pre_act = pre_act + out_bias[:, None]
    layer_out = gelu_tanh(pre_act).astype(jnp.bfloat16)
    grad_pre = jax.vjp(gelu_tanh, pre_act)[1](out_cotangent.astype(jnp.float32))[0].astype(
        jnp.bfloat16
    )
    shard_piece = lax.all_gather(grad_pre, "feat", axis=0, tiled=True)
    self_term = lax.dot_general(
        node_feats, shard_piece, (((1,), (1,)), ((), ())), preferred_element_type=jnp.float32
    )
    neigh_term = lax.dot_general(
        aggregate, shard_piece, (((1,), (1,)), ((), ())), preferred_element_type=jnp.float32
    )
    grad_w_self = self_term
    grad_w_neigh = neigh_term
    self_back = jnp.dot(weight_self, shard_piece, preferred_element_type=jnp.float32)
    neigh_back = jnp.dot(weight_neigh, shard_piece, preferred_element_type=jnp.float32)
    grad_w_self, grad_w_neigh, self_grad, neigh_back = (
        grad_w_self,
        grad_w_neigh,
        self_back,
        neigh_back,
    )
    agg_grad = neigh_back.reshape(local_width, NBLK, BLK) / divisor[None]
    bias_term = jnp.sum(grad_pre, axis=1, dtype=jnp.float32)
    grad_w_self, grad_w_neigh, bias_total = lax.psum((grad_w_self, grad_w_neigh, bias_term), "dom")
    scale = 1.0 / jnp.sqrt(jnp.float32(ROWS * num_parts))
    grad_self = grad_w_self * scale
    grad_neigh = grad_w_neigh * scale
    grad_bias = bias_total * scale
    picked_grad = agg_grad[:, my_rows]
    contrib = jnp.einsum(
        "ftr,trc->ftc", picked_grad, my_tiles.astype(jnp.float32), precision=highest
    )
    cols_hot = jax.nn.one_hot(my_cols, ext_blocks, dtype=jnp.float32) * live[:, None]
    ext_grad = jnp.einsum("ftc,tn->fnc", contrib, cols_hot, precision=highest)
    halo_grad = ext_grad[:, NBLK:].reshape(local_width, num_parts * CAP * BLK)
    returned = lax.all_to_all(halo_grad, "dom", split_axis=1, concat_axis=1, tiled=True)
    send_hot = jax.nn.one_hot(my_sends, NBLK, dtype=jnp.float32)
    gathered_back = jnp.einsum(
        "fsc,sb->fbc",
        returned.reshape(local_width, num_parts * CAP, BLK),
        send_hot,
        precision=highest,
    )
    total = self_grad.reshape(local_width, NBLK, BLK) + ext_grad[:, :NBLK] + gathered_back
    feats_grad = total.astype(jnp.bfloat16).reshape(local_width, ROWS)
    return (layer_out, feats_grad, grad_self, grad_neigh, grad_bias)


def solution(mesh):
    in_specs = (
        P("feat", "dom"),
        P("feat", "dom"),
        P("feat", None),
        P("feat", None),
        P("feat"),
        P("dom", None, None),
        P("dom", None),
        P("dom", None),
        P("dom"),
        P("dom", None, None, None),
    )
    out_specs = (P("feat", "dom"), P("feat", "dom"), P("feat", None), P("feat", None), P("feat"))
    return jax.shard_map(
        per_device, mesh=mesh, in_specs=in_specs, out_specs=out_specs, check_vma=False
    )
```

profile of v0, /device:TPU:2, one launch (start us, length us, event | category | flops | bytes accessed | tf_op | source)
XLA Modules:
  0.0 411.8 jit_solution(10953175642827898887)
XLA Ops:
  8.7 0.8 copy.39
  10.3 1.6 gather_fusion
  12.1 0.8 copy.42
  12.9 15.2 %all-to-all-start.1 = ((bf16[32,16,256]{2,0,1:T(8,128)(2,1)}), bf16[32,16,256]{2,0,1:T(8,128)(2,1)S(1)}, u32[]{:S(2)}, u32[]{:S(2)}) async-start(bf16[32,16,256]{2,0,1:T(8,128)(2,1)} %copy.42), calls=%async_computation.1 | async-start | bytes 524288 | tf_op jit(solution)/shard_map/all_to_all | solution.py:46
  29.6 16.9 %all-to-all-done.1 = bf16[32,16,256]{2,0,1:T(8,128)(2,1)S(1)} async-done(((bf16[32,16,256]{2,0,1:T(8,128)(2,1)}), bf16[32,16,256]{2,0,1:T(8,128)(2,1)S(1)}, u32[]{:S(2)}, u32[]{:S(2)}) %all-to-all-start.1) | async-done | bytes 262176 | tf_op jit(solution)/shard_map/all_to_all | solution.py:46
  46.5 7.7 %all-to-all-start = ((bf16[32,32,128]{2,0,1:T(8,128)(2,1)}), bf16[32,32,128]{2,0,1:T(8,128)(2,1)}, u32[]{:S(2)}, u32[]{:S(2)}) async-start(bf16[32,32,128]{2,0,1:T(8,128)(2,1)} %copy_bitcast_fusion.1), calls=%async_computation | async-start | bytes 524288 | tf_op jit(solution)/shard_map/all_to_all | solution.py:60
  54.5 1.0 pad_maximum_fusion
  56.2 1.2 fusion.4
  57.4 1.2 fusion.12
  59.3 0.8 copy.47
  60.1 1.8 all-to-all-done
  61.9 5.6 %all-to-all-start.2 = ((bf16[32,32,128]{2,0,1:T(8,128)(2,1)}), bf16[32,32,128]{2,0,1:T(8,128)(2,1)S(1)}, u32[]{:S(2)}, u32[]{:S(2)}) async-start(bf16[32,32,128]{2,0,1:T(8,128)(2,1)} %copy.47), calls=%async_computation.2 | async-start | bytes 524288 | tf_op jit(solution)/shard_map/all_to_all | solution.py:61
  67.6 7.1 %all-gather.4.cloned.1.call-done = bf16[1024,1024]{1,0:T(8,128)(2,1)} async-done(((bf16[32,1024]{1,0:T(8,128)(2,1)}), bf16[1024,1024]{1,0:T(8,128)(2,1)}) %all-gather.4.cloned.1.call-update) | async-done | bytes 2097168 | tf_op jit(solution)/shard_map/all_gather | solution.py:63
  74.7 2.3 fusion.54
  77.1 60.3 %all-gather.6.cloned.1.call-done = bf16[1024,1024]{1,0:T(8,128)(2,1)} async-done(((bf16[32,1024]{1,0:T(8,128)(2,1)}), bf16[1024,1024]{1,0:T(8,128)(2,1)}) %all-gather.6.cloned.1.call-update) | async-done | bytes 2097168 | tf_op jit(solution)/shard_map/all_gather | solution.py:65
  137.4 2.6 fusion.10
  140.0 15.6 %all_to_all.72 = f32[32,32,128]{2,1,0:T(8,128)S(1)} all-to-all(f32[32,32,128]{2,1,0:T(8,128)S(1)} %bitcast.119), channel_id=1, replica_groups=mesh['dom'=16,'feat'=32] {'feat'}, dimensions={0} | all-to-all | bytes 1048576 | tf_op jit(solution)/shard_map/all_to_all | solution.py:67
  155.6 1.4 convert_reduce_fusion.1
  157.0 67.5 %all-gather.8.cloned.1.call-done = bf16[1024,4096]{1,0:T(8,128)(2,1)} async-done(((bf16[32,4096]{1,0:T(8,128)(2,1)}), bf16[1024,4096]{1,0:T(8,128)(2,1)}) %all-gather.8.cloned.1.call-update) | async-done | bytes 8388624 | tf_op jit(solution)/shard_map/all_gather | solution.py:73
  224.6 5.1 %convolution_bitcast_fusion.1 = f32[4,32,8,128]{3,2,1,0:T(8,128)S(1)} fusion(bf16[32,1024]{1,0:T(8,128)(2,1)S(1)} %copy-done.5, bf16[1024,4096]{1,0:T(8,128)(2,1)} %all-gather.8.cloned.1.call-done), kind=kOutput, calls=%fused_computation.11 | convolution fusion | flops 268435456 | bytes 8978432 | tf_op jit(solution)/shard_map/dot_general | solution.py:83
  230.4 1.5 convolution_bitcast_fusion.2
  232.0 1.7 gather_fusion.2
  233.7 3.0 fusion.7
  236.6 1.6 convolution_bitcast_fusion
  238.6 1.2 copy.53
  239.7 12.3 %all-to-all-start.4 = ((f32[32,16,256]{2,0,1:T(8,128)}), f32[32,16,256]{2,0,1:T(8,128)S(1)}, u32[]{:S(2)}, u32[]{:S(2)}) async-start(f32[32,16,256]{2,0,1:T(8,128)} %copy.53), calls=%async_computation.4 | async-start | bytes 1048576 | tf_op jit(solution)/shard_map/all_to_all | solution.py:104
  252.1 6.7 %convolution_bitcast_fusion.5 = f32[32,1024]{1,0:T(8,128)} fusion(bf16[1024,4096]{1,0:T(8,128)(2,1)} %all-gather.8.cloned.1.call-done, bf16[32,4096]{1,0:T(8,128)(2,1)S(1)} %copy-done), kind=kOutput, calls=%fused_computation.20 | convolution fusion | flops 268435456 | bytes 8781824 | tf_op jit(solution)/shard_map/dot_general | solution.py:74
  258.7 6.6 %fusion.28 = f32[32,1024]{1,0:T(8,128)} fusion(bf16[1024,4096]{1,0:T(8,128)(2,1)} %all-gather.8.cloned.1.call-done, bf16[4,8,32,128]{3,2,1,0:T(8,128)(2,1)S(1)} %bitcast.121), kind=kOutput, calls=%fused_computation.46 | convolution fusion | flops 268435456 | bytes 8781824 | tf_op jit(solution)/shard_map/dot_general | solution.py:77
  265.5 35.6 %psum.23 = f32[32]{0:T(128)S(1)} all-reduce(f32[32]{0:T(128)S(1)} %get-tuple-element.7), channel_id=1, replica_groups=mesh['dom'=16,'feat'=32] {'dom'}, use_global_device_ids=true, to_apply=%region_4.5 | all-reduce | flops 32 | bytes 256 | tf_op jit(solution)/shard_map/psum | solution.py:92
  301.6 100.4 %all-reduce.3.cloned.1.call-done = (f32[32,1024]{1,0:T(8,128)}, f32[32,1024]{1,0:T(8,128)}) async-done(((f32[32,1024]{1,0:T(8,128)}, f32[32,1024]{1,0:T(8,128)}), (f32[32,1024]{1,0:T(8,128)}, f32[32,1024]{1,0:T(8,128)})) %all-reduce.3.cloned.1.call-update) | async-done | bytes 262160 | tf_op jit(solution)/shard_map/psum | solution.py:92
  402.0 1.7 broadcast_multiply_fusion
  404.4 0.8 copy.85
  (58 shorter events, 7.5 us)
Async XLA Ops:
  7.2 2.4 copy-start
  7.2 21.6 %copy-start.10 = (s32[1,64]{1,0:T(1,128)S(1)}, s32[1,64]{1,0:T(1,128)}, u32[]{:S(2)}) copy-start(s32[1,64]{1,0:T(1,128)} %param.17) | copy-start | bytes 772
  7.2 21.6 %copy-start.2 = (bf16[1,64,128,128]{3,2,1,0:T(8,128)(2,1)S(1)}, bf16[1,64,128,128]{3,2,1,0:T(8,128)(2,1)}, u32[]{:S(2)}) copy-start(bf16[1,64,128,128]{3,2,1,0:T(8,128)(2,1)} %param.19) | copy-start | bytes 6291460
  7.2 67.5 %all-gather.4.cloned.1.call-start = ((), (), s32[]{:S(2)}) async-start(), calls=%async_computation.5 | async-start | bytes 2162688 | tf_op jit(solution)/shard_map/all_gather | solution.py:63
  7.9 129.4 %all-gather.6.cloned.1.call-start = ((), (), s32[]{:S(2)}) async-start(), calls=%async_computation.6 | async-start | bytes 2162688 | tf_op jit(solution)/shard_map/all_gather | solution.py:65
  11.9 17.5 %copy-start.9 = (s32[1,64]{1,0:T(1,128)S(1)}, s32[1,64]{1,0:T(1,128)}, u32[]{:S(2)}) copy-start(s32[1,64]{1,0:T(1,128)} %param.16) | copy-start | bytes 772
  12.9 33.6 %all-to-all-start.1 = ((bf16[32,16,256]{2,0,1:T(8,128)(2,1)}), bf16[32,16,256]{2,0,1:T(8,128)(2,1)S(1)}, u32[]{:S(2)}, u32[]{:S(2)}) async-start(bf16[32,16,256]{2,0,1:T(8,128)(2,1)} %copy.42), calls=%async_computation.1 | async-start | bytes 524288 | tf_op jit(solution)/shard_map/all_to_all | solution.py:46
  46.5 15.4 %all-to-all-start = ((bf16[32,32,128]{2,0,1:T(8,128)(2,1)}), bf16[32,32,128]{2,0,1:T(8,128)(2,1)}, u32[]{:S(2)}, u32[]{:S(2)}) async-start(bf16[32,32,128]{2,0,1:T(8,128)(2,1)} %copy_bitcast_fusion.1), calls=%async_computation | async-start | bytes 524288 | tf_op jit(solution)/shard_map/all_to_all | solution.py:60
  58.6 0.7 copy-start.3
  61.9 15.2 %all-to-all-start.2 = ((bf16[32,32,128]{2,0,1:T(8,128)(2,1)}), bf16[32,32,128]{2,0,1:T(8,128)(2,1)S(1)}, u32[]{:S(2)}, u32[]{:S(2)}) async-start(bf16[32,32,128]{2,0,1:T(8,128)(2,1)} %copy.47), calls=%async_computation.2 | async-start | bytes 524288 | tf_op jit(solution)/shard_map/all_to_all | solution.py:61
  67.5 157.1 %all-gather.8.cloned.1.call-start = ((), (), s32[]{:S(2)}) async-start(), calls=%async_computation.7 | async-start | bytes 8650752 | tf_op jit(solution)/shard_map/all_gather | solution.py:73
  137.4 18.2 %copy-start.7 = (bf16[32,4096]{1,0:T(8,128)(2,1)S(1)}, bf16[32,4096]{1,0:T(8,128)(2,1)}, u32[]{:S(2)}) copy-start(bf16[32,4096]{1,0:T(8,128)(2,1)} %param.11) | copy-start | bytes 786436
  137.4 18.2 %copy-start.8 = (f32[32]{0:T(128)S(1)}, f32[32]{0:T(128)}, u32[]{:S(2)}) copy-start(f32[32]{0:T(128)} %param.14) | copy-start | bytes 388
  140.0 84.6 %copy-start.5 = (bf16[32,1024]{1,0:T(8,128)(2,1)S(1)}, bf16[32,1024]{1,0:T(8,128)(2,1)}, u32[]{:S(2)}) copy-start(bf16[32,1024]{1,0:T(8,128)(2,1)} %param.13) | copy-start | bytes 196612
  157.0 72.7 %copy-start.6 = (bf16[32,1024]{1,0:T(8,128)(2,1)S(1)}, bf16[32,1024]{1,0:T(8,128)(2,1)}, u32[]{:S(2)}) copy-start(bf16[32,1024]{1,0:T(8,128)(2,1)} %param.12) | copy-start | bytes 196612
  224.6 5.8 %copy-start.1 = (bf16[1024,4096]{1,0:T(8,128)(2,1)S(1)}, bf16[1024,4096]{1,0:T(8,128)(2,1)}, u32[]{:S(2)}) copy-start(bf16[1024,4096]{1,0:T(8,128)(2,1)} %all-gather.8.cloned.1.call-done) | copy-start | bytes 25165828
  239.7 164.0 %all-to-all-start.4 = ((f32[32,16,256]{2,0,1:T(8,128)}), f32[32,16,256]{2,0,1:T(8,128)S(1)}, u32[]{:S(2)}, u32[]{:S(2)}) async-start(f32[32,16,256]{2,0,1:T(8,128)} %copy.53), calls=%async_computation.4 | async-start | bytes 1048576 | tf_op jit(solution)/shard_map/all_to_all | solution.py:104
  252.0 6.7 %copy-start.4 = (bf16[32,32,128]{2,0,1:T(8,128)(2,1)S(1)}, bf16[32,32,128]{2,0,1:T(8,128)(2,1)}, u32[]{:S(2)}) copy-start(bf16[32,32,128]{2,0,1:T(8,128)(2,1)} %copy-done.3) | copy-start | bytes 786436
  252.0 150.0 %all-reduce.3.cloned.1.call-start = ((), (), s32[]{:S(2)}) async-start(), calls=%async_computation.8 | async-start | bytes 524288 | tf_op jit(solution)/shard_map/psum | solution.py:92
Sparse Core Ops, SparseCore 0:
  11.1 63.5 all-gather.3
  77.9 59.4 all-gather.5
  157.1 67.4 all-gather.7
  265.5 136.4 all-reduce.2
where the time goes:
time: 413 us; the launch traced here: 412 us
  waiting for transfers between devices  256 us (62%)
  blocking collectives  51.2 us (12%)
  starting transfers between devices  40.9 us (10%)
  matrix products  32.3 us (8%)
  between operations  14.8 us (4%)
  local copies, waits for them, and re-layouts  11.6 us (3%)
  other arithmetic  5.43 us (1%)
    psum x1, waiting for transfers between devices, per_device(): lax.psum((grad_w_self, grad_w_neigh, bias_term), 'dom')  100 us
    all_gather x1, waiting for transfers between devices, per_device(): shard_piece = lax.all_gather(grad_pre, 'feat', axis=0, tiled=True)  67.5 us
    all_gather x1, waiting for transfers between devices, per_device(): lax.all_gather(weight_neigh, 'feat', axis=0, tiled=True)  60.3 us
    psum x1, blocking collectives, per_device(): lax.psum((grad_w_self, grad_w_neigh, bias_term), 'dom')  35.6 us
    all_to_all x1, waiting for transfers between devices, per_device(): lax.all_to_all(outgoing, 'dom', split_axis=1, concat_axis=1, tiled=True)  16.9 us
    all_to_all x1, blocking collectives, per_device(): lax.all_to_all(out_by_rows, 'feat', split_axis=0, concat_axis=1, tiled=True)  15.6 us
    all_to_all x1, starting transfers between devices, per_device(): lax.all_to_all(outgoing, 'dom', split_axis=1, concat_axis=1, tiled=True)  15.2 us
    all_to_all x1, starting transfers between devices, per_device(): lax.all_to_all(halo_grad, 'dom', split_axis=1, concat_axis=1, tiled=True)  12.3 us
  transfers between devices with their start and end apart: 8, of which 6 were waited for; matrix products, arithmetic and copies ran while one was open for 7% of the time, Pallas kernels for 0%

commit v1 on v0

v1 whole, which is shorter than its diff:
```python
import jax
import jax.numpy as jnp
from jax import lax
from jax.experimental import pallas as pl
from jax.experimental.pallas import tpu as pltpu
from jax.sharding import PartitionSpec as P

BLK = 128
NBLK = 32
CAP = 2
TMAX = 64
ROWS = 4096
UNROLL = 8

SMEM = pl.BlockSpec(memory_space=pltpu.SMEM)
VMEM = pl.BlockSpec(memory_space=pltpu.VMEM)
PAIRS = [(i, i ^ 1) for i in range(32)]


def lanes(block):
    return pl.ds(pl.multiple_of(block * BLK, BLK), BLK)


def outgoing_kernel(sends, feats, out):
    for slot in range(out.shape[0] * CAP):
        part, place = divmod(slot, CAP)
        out[part, :, place * BLK : (place + 1) * BLK] = feats[:, lanes(sends[slot])]


def aggregate_kernel(rows, cols, count, feats, halo, tiles, out, divisor, ext, acc):
    width = feats.shape[0]
    ones = jnp.ones((16, BLK), jnp.bfloat16)
    for block in range(NBLK):
        ext[block, :width] = feats[:, block * BLK : (block + 1) * BLK]
        ext[block, width:] = ones
    for slot in range(halo.shape[0] * CAP):
        part, place = divmod(slot, CAP)
        ext[NBLK + slot, :width] = halo[part, :, place * BLK : (place + 1) * BLK]
        ext[NBLK + slot, width:] = ones
    acc[...] = jnp.zeros_like(acc)
    live = count[0]

    def step(group, carry):
        for inner in range(UNROLL):
            slot = group * UNROLL + inner
            alive = slot < live
            source = jnp.where(alive, cols[slot], 0)
            target = jnp.where(alive, rows[slot], NBLK)
            acc[target] += lax.dot_general(
                ext[source], tiles[slot], (((1,), (1,)), ((), ())), preferred_element_type=jnp.float32
            )
        return carry

    lax.fori_loop(0, (live + UNROLL - 1) // UNROLL, step, 0)
    for block in range(NBLK):
        chip, core = divmod(block, 2)
        span = slice(core * BLK, (core + 1) * BLK)
        div = jnp.maximum(acc[block, width : width + 1], 1.0)
        divisor[block : block + 1] = div
        out[2 * chip, :, span] = feats[:, block * BLK : (block + 1) * BLK]
        out[2 * chip + 1, :, span] = (acc[block, :width] / div).astype(jnp.bfloat16)


def scatter_kernel(rows, cols, count, back, divisor, tiles, halo, own, scaled, acc):
    width = own.shape[0]
    for block in range(NBLK):
        chip, core = divmod(block, 2)
        span = slice(core * BLK, (core + 1) * BLK)
        scaled[block] = (
            back[2 * chip + 1, :, span].astype(jnp.float32) / divisor[block : block + 1]
        ).astype(jnp.bfloat16)
        acc[block] = back[2 * chip, :, span].astype(jnp.float32)
    acc[NBLK:] = jnp.zeros((acc.shape[0] - NBLK, width, BLK), jnp.float32)
    live = count[0]
    spare = acc.shape[0] - 1

    def step(group, carry):
        for inner in range(UNROLL):
            slot = group * UNROLL + inner
            alive = slot < live
            source = jnp.where(alive, rows[slot], 0)
            target = jnp.where(alive, cols[slot], spare)
            acc[target] += jnp.dot(scaled[source], tiles[slot], preferred_element_type=jnp.float32)
        return carry

    lax.fori_loop(0, (live + UNROLL - 1) // UNROLL, step, 0)
    for block in range(NBLK):
        own[:, block * BLK : (block + 1) * BLK] = acc[block]
    for slot in range(halo.shape[0] * CAP):
        part, place = divmod(slot, CAP)
        halo[part, :, place * BLK : (place + 1) * BLK] = acc[NBLK + slot].astype(jnp.bfloat16)


def collect_kernel(sends, own, returned, out, acc):
    acc[...] = own[...]
    for slot in range(returned.shape[0] * CAP):
        part, place = divmod(slot, CAP)
        spot = lanes(sends[slot])
        acc[:, spot] += returned[part, :, place * BLK : (place + 1) * BLK].astype(jnp.float32)
    out[...] = acc[...].astype(jnp.bfloat16)


def pieces(values):
    high = lax.reduce_precision(values, 8, 7)
    rest = values - high
    middle = lax.reduce_precision(rest, 8, 7)
    low = rest - middle
    return jnp.stack([high, middle, low], axis=-1).astype(jnp.bfloat16)


def gelu_and_slope(v):
    root = 0.7978845608028654
    t = jnp.tanh(root * (v + 0.044715 * v * v * v))
    value = 0.5 * v * (1.0 + t)
    slope = 0.5 * (1.0 + t) + 0.5 * v * (1.0 - t * t) * (root * (1.0 + 3 * 0.044715 * v * v))
    return value, slope


def swap(values, axis):
    return lax.all_to_all(values, axis, split_axis=0, concat_axis=0, tiled=True)


def per_device(
    node_feats,
    out_cotangent,
    weight_self,
    weight_neigh,
    out_bias,
    send_blocks,
    tile_rows,
    tile_cols,
    tile_count,
    tile_values,
):
    f32, bf16 = jnp.float32, jnp.bfloat16
    width = node_feats.shape[0]
    parts = lax.axis_size("dom")
    shards = lax.axis_size("feat")
    dims = width * shards
    core = lax.axis_index("feat") % 2
    sends = send_blocks[0].reshape(parts * CAP)
    rows, cols, tiles = tile_rows[0], tile_cols[0], tile_values[0]

    outgoing = pl.pallas_call(
        outgoing_kernel,
        out_shape=jax.ShapeDtypeStruct((parts, width, CAP * BLK), bf16),
        in_specs=[SMEM, VMEM],
        out_specs=VMEM,
        name="outgoing",
    )(sends, node_feats)
    halo = swap(outgoing, "dom")

    both = jnp.stack([weight_self, weight_neigh])
    both = jnp.broadcast_to(both[None], (shards // 2, 2, width, dims)).reshape(shards, width, dims)
    cot = jnp.transpose(out_cotangent.reshape(width, NBLK, BLK), (1, 0, 2))
    bias = jnp.pad(pieces(out_bias), ((0, 0), (0, BLK - 3)))
    bias = jnp.broadcast_to(bias[None], (shards, width, BLK))
    packed = swap(jnp.concatenate([both, cot, bias], axis=2), "feat")
    packed = packed.reshape(dims, dims + 2 * BLK)
    weight = packed[:, :dims]
    cot = packed[:, dims : dims + BLK].astype(f32)
    bias = jnp.sum(packed[:, dims + BLK : dims + BLK + 3].astype(f32), axis=1, keepdims=True)

    spread, divisor = pl.pallas_call(
        aggregate_kernel,
        out_shape=(
            jax.ShapeDtypeStruct((shards, width, 2 * BLK), bf16),
            jax.ShapeDtypeStruct((NBLK, BLK), f32),
        ),
        in_specs=[SMEM, SMEM, SMEM, VMEM, VMEM, VMEM],
        out_specs=(VMEM, VMEM),
        scratch_shapes=[
            pltpu.VMEM((NBLK + parts * CAP, width + 16, BLK), bf16),
            pltpu.VMEM((NBLK + 1, width + 16, BLK), f32),
        ],
        name="aggregate",
    )(rows, cols, tile_count, node_feats, halo, tiles)
    data = swap(spread, "feat").reshape(dims, 2 * BLK)

    product = lax.dot_general(weight, data, (((0,), (0,)), ((), ())), preferred_element_type=f32)
    keep = lax.dynamic_slice(product, (0, core * BLK), (dims, BLK))
    send = lax.dynamic_slice(product, (0, (1 - core) * BLK), (dims, BLK))
    pre_act = keep + lax.ppermute(send, "feat", PAIRS) + bias
    value, slope = gelu_and_slope(pre_act)
    layer = value.astype(bf16)
    grad = (cot * slope).astype(bf16)
    other = lax.ppermute(grad, "feat", PAIRS)
    grads = jnp.where(
        core == 0, jnp.concatenate([grad, other], 1), jnp.concatenate([other, grad], 1)
    )
    back = jnp.dot(weight, grads, preferred_element_type=f32).astype(bf16)
    back = swap(back.reshape(shards, width, 2 * BLK), "feat")

    term = lax.dot_general(data, grads, (((1,), (1,)), ((), ())), preferred_element_type=f32)
    bias_sum = jnp.pad(pieces(jnp.sum(grad.astype(f32), axis=1)), ((0, 0), (0, BLK - 3)))
    joined = jnp.concatenate([term.astype(bf16), layer, bias_sum], axis=1)
    joined = swap(joined.reshape(shards, width, dims + 2 * BLK), "feat")
    layer_out = jnp.transpose(joined[:, :, dims : dims + BLK], (1, 0, 2)).reshape(width, ROWS)
    sums = jnp.sum(
        joined[:, :, :dims].reshape(shards // 2, 2, width, dims).astype(f32), axis=0
    )
    bias_part = jnp.sum(joined[:, :, dims + BLK : dims + BLK + 3].astype(f32), axis=(0, 2))

    halo_grad, own = pl.pallas_call(
        scatter_kernel,
        out_shape=(
            jax.ShapeDtypeStruct((parts, width, CAP * BLK), bf16),
            jax.ShapeDtypeStruct((width, ROWS), f32),
        ),
        in_specs=[SMEM, SMEM, SMEM, VMEM, VMEM, VMEM],
        out_specs=(VMEM, VMEM),
        scratch_shapes=[
            pltpu.VMEM((NBLK, width, BLK), bf16),
            pltpu.VMEM((NBLK + parts * CAP + 1, width, BLK), f32),
        ],
        name="scatter",
    )(rows, cols, tile_count, back, divisor, tiles)
    returned = swap(halo_grad, "dom")
    feats_grad = pl.pallas_call(
        collect_kernel,
        out_shape=jax.ShapeDtypeStruct((width, ROWS), bf16),
        in_specs=[SMEM, VMEM, VMEM],
        out_specs=VMEM,
        scratch_shapes=[pltpu.VMEM((width, ROWS), f32)],
        name="collect",
    )(sends, own, returned)

    chunk = 2 * dims // parts
    cut = jnp.transpose(sums.reshape(2, width, parts // 2, chunk), (0, 2, 1, 3))
    cut = cut.reshape(parts, width, chunk).astype(bf16)
    extra = jnp.pad(pieces(bias_part).T, ((0, 13), (0, BLK - width)))
    cut = jnp.concatenate([cut, jnp.broadcast_to(extra[None], (parts, 16, BLK))], axis=1)
    cut = swap(cut, "dom").astype(f32)
    scale = 1.0 / jnp.sqrt(f32(ROWS * parts))
    piece = jnp.sum(cut[:, :width], axis=0) * scale
    grad_bias = jnp.sum(cut[:, width : width + 3, :width], axis=(0, 1)) * scale
    whole = swap(jnp.broadcast_to(piece[None], (parts, width, chunk)), "dom")
    whole = jnp.transpose(whole.reshape(2, parts // 2, width, chunk), (0, 2, 1, 3))
    whole = whole.reshape(2, width, dims)
    return (layer_out, feats_grad, whole[0], whole[1], grad_bias)


def solution(mesh):
    in_specs = (
        P("feat", "dom"),
        P("feat", "dom"),
        P("feat", None),
        P("feat", None),
        P("feat"),
        P("dom", None, None),
        P("dom", None),
        P("dom", None),
        P("dom"),
        P("dom", None, None, None),
    )
    out_specs = (P("feat", "dom"), P("feat", "dom"), P("feat", None), P("feat", None), P("feat"))
    return jax.shard_map(
        per_device, mesh=mesh, in_specs=in_specs, out_specs=out_specs, check_vma=False
    )
```

time: 413 us -> 240 us (0.58)
  the two profiles are of different devices: /device:TPU:2 before, /device:TPU:32 now
where the time goes in v1:
time: 240 us; the launch traced here: 239 us
  waiting for transfers between devices  143 us (60%)
  starting transfers between devices  57.8 us (24%)
  local copies, waits for them, and re-layouts  13 us (5%)
  Pallas kernels  10.4 us (4%)
  other arithmetic  8.83 us (4%)
  matrix products  4.31 us (2%)
    all_to_all x8, waiting for transfers between devices, swap(): return lax.all_to_all(values, axis, split_axis=0, concat_axis=0, tiled=True)  141 us
    all_to_all x8, starting transfers between devices, swap(): return lax.all_to_all(values, axis, split_axis=0, concat_axis=0, tiled=True)  53.9 us
  transfers between devices with their start and end apart: 10, of which 10 were waited for; matrix products, arithmetic and copies ran while one was open for 6% of the time, Pallas kernels for 2%

profile of v1, /device:TPU:32, one launch (start us, length us, event | category | flops | bytes accessed | tf_op | source)
XLA Modules:
  0.0 239.0 jit_solution(2922889981773992456)
XLA Ops:
  2.0 1.7 outgoing.1
  3.8 15.3 %all-to-all-start = ((bf16[16,32,256]{2,1,0:T(8,128)(2,1)}), bf16[16,32,256]{2,1,0:T(8,128)(2,1)S(1)}, u32[]{:S(2)}, u32[]{:S(2)}) async-start(bf16[16,32,256]{2,1,0:T(8,128)(2,1)} %outgoing.1), calls=%async_computation | async-start | bytes 524288 | tf_op jit(solution)/shard_map/all_to_all | solution.py:120
  20.4 16.6 %all-to-all-done.halo = bf16[16,32,256]{2,1,0:T(8,128)(2,1)S(1)} async-done(((bf16[16,32,256]{2,1,0:T(8,128)(2,1)}), bf16[16,32,256]{2,1,0:T(8,128)(2,1)S(1)}, u32[]{:S(2)}, u32[]{:S(2)}) %all-to-all-start) | async-done | bytes 262176 | tf_op jit(solution)/shard_map/all_to_all | solution.py:120
  37.7 3.4 %aggregate.1 = (bf16[32,32,256]{2,1,0:T(8,128)(2,1)}, f32[32,128]{1,0:T(8,128)}) custom-call(s32[64]{0:T(128)} %bitcast.82, s32[64]{0:T(128)} %bitcast.84, s32[1]{0:T(128)S(6)} %copy.42.count, bf16[32,4096]{1,0:T(8,128)(2,1)} %feats.3, bf16[16,32,256]{2,1,0:T(8,128)(2,1)} %copy-done.4, bf16[64,128,128]{2,1,0:T(8,128)(2,1)} %bitcast.60), custom_call_target="tpu_custom_call" | custom-call | tf_op jit(solution)/shard_map/aggregate/pallas_call | solution.py:164
  41.2 7.3 %all-to-all-start.1 = ((bf16[32,32,256]{2,1,0:T(8,128)(2,1)}), bf16[32,32,256]{2,1,0:T(8,128)(2,1)S(1)}, u32[]{:S(2)}, u32[]{:S(2)}) async-start(bf16[32,32,256]{2,1,0:T(8,128)(2,1)} %get-tuple-element.9), calls=%async_computation.1 | async-start | bytes 1048576 | tf_op jit(solution)/shard_map/all_to_all | solution.py:120
  49.1 1.8 pad_maximum_fusion
  51.0 8.6 %all-to-all-done.1 = bf16[32,32,256]{2,1,0:T(8,128)(2,1)S(1)} async-done(((bf16[32,32,256]{2,1,0:T(8,128)(2,1)}), bf16[32,32,256]{2,1,0:T(8,128)(2,1)S(1)}, u32[]{:S(2)}, u32[]{:S(2)}) %all-to-all-start.1) | async-done | bytes 524320 | tf_op jit(solution)/shard_map/all_to_all | solution.py:120
  59.6 4.1 %all-to-all-start.2 = ((bf16[32,32,1280]{2,1,0:T(8,128)(2,1)}), bf16[32,32,1280]{2,1,0:T(8,128)(2,1)S(1)}, u32[]{:S(2)}, u32[]{:S(2)}) async-start(bf16[32,32,1280]{2,1,0:T(8,128)(2,1)} %pad_maximum_fusion), calls=%async_computation.2 | async-start | bytes 5242880 | tf_op jit(solution)/shard_map/all_to_all | solution.py:120
  63.7 34.6 %all-to-all-done.2 = bf16[32,32,1280]{2,1,0:T(8,128)(2,1)S(1)} async-done(((bf16[32,32,1280]{2,1,0:T(8,128)(2,1)}), bf16[32,32,1280]{2,1,0:T(8,128)(2,1)S(1)}, u32[]{:S(2)}, u32[]{:S(2)}) %all-to-all-start.2) | async-done | bytes 2621472 | tf_op jit(solution)/shard_map/all_to_all | solution.py:120
  99.0 1.0 copy-done.3
  100.9 1.9 collective-permute-start
  103.8 1.2 collective-permute-done
  105.0 2.4 %convert_reduce_fusion.1 = (f32[1024]{0:T(1024)S(1)}, bf16[1024,128]{0,1:T(8,128)(2,1)S(1)}, bf16[1024,128]{0,1:T(8,128)(2,1)}) fusion(f32[1024]{0:T(1024)S(1)} %convert_reduce_fusion.2, f32[1024,128]{0,1:T(8,128)} %collective-permute-done, f32[1024,256]{0,1:T(8,128)} %copy-done.3, s32[]{:T(128)S(6)} %select_n.23, bf16[1024,128]{0,1:T(8,128)(2,1)} %copy.32), kind=kLoop, calls=%fused_computation.24 | loop fusion | flops 3406848 | bytes 1843204 | tf_op jit(solution)/shard_map/reduce_sum | solution.py:195
  107.4 2.0 collective-permute-start.1
  109.5 1.3 collective-permute-done.1
  110.8 1.6 fusion.4
  112.4 3.9 %all-to-all-start.4 = ((bf16[32,32,256]{2,1,0:T(8,128)(2,1)}), bf16[32,32,256]{2,1,0:T(8,128)(2,1)S(1)}, u32[]{:S(2)}, u32[]{:S(2)}) async-start(bf16[32,32,256]{2,1,0:T(8,128)(2,1)} %bitcast.74), calls=%async_computation.4 | async-start | bytes 1048576 | tf_op jit(solution)/shard_map/all_to_all | solution.py:120
  116.3 2.0 convolution_convert_fusion
  118.6 2.7 %copy.27 = bf16[1024,1280]{1,0:T(8,128)(2,1)} copy(bf16[1024,1280]{0,1:T(8,128)(2,1)S(1)} %pad_maximum_fusion.1) | data formatting | bytes 5242880 | tf_op jit(solution)/shard_map/concatenate | solution.py:196
  121.3 6.1 %all-to-all-done.4.back = bf16[32,32,256]{2,1,0:T(8,128)(2,1)S(1)} async-done(((bf16[32,32,256]{2,1,0:T(8,128)(2,1)}), bf16[32,32,256]{2,1,0:T(8,128)(2,1)S(1)}, u32[]{:S(2)}, u32[]{:S(2)}) %all-to-all-start.4) | async-done | bytes 524320 | tf_op jit(solution)/shard_map/all_to_all | solution.py:120
  128.2 4.1 %all-to-all-start.3 = ((bf16[32,32,1280]{2,1,0:T(8,128)(2,1)}), bf16[32,32,1280]{2,1,0:T(8,128)(2,1)S(1)}, u32[]{:S(2)}, u32[]{:S(2)}) async-start(bf16[32,32,1280]{2,1,0:T(8,128)(2,1)} %bitcast.59), calls=%async_computation.3 | async-start | bytes 5242880 | tf_op jit(solution)/shard_map/all_to_all | solution.py:120
  132.3 3.2 %scatter.1 = (bf16[16,32,256]{2,1,0:T(8,128)(2,1)}, f32[32,4096]{1,0:T(8,128)}) custom-call(s32[64]{0:T(128)} %bitcast.83, s32[64]{0:T(128)} %bitcast.85, s32[1]{0:T(128)S(6)} %copy.42.count, bf16[32,32,256]{2,1,0:T(8,128)(2,1)} %copy-done, f32[32,128]{1,0:T(8,128)} %get-tuple-element.10.divisor, bf16[64,128,128]{2,1,0:T(8,128)(2,1)} %bitcast.61), custom_call_target="tpu_custom_call" | custom-call | tf_op jit(solution)/shard_map/scatter/pallas_call | solution.py:204
  135.5 31.4 %all-to-all-done.3 = bf16[32,32,1280]{2,1,0:T(8,128)(2,1)S(1)} async-done(((bf16[32,32,1280]{2,1,0:T(8,128)(2,1)}), bf16[32,32,1280]{2,1,0:T(8,128)(2,1)S(1)}, u32[]{:S(2)}, u32[]{:S(2)}) %all-to-all-start.3) | async-done | bytes 2621472 | tf_op jit(solution)/shard_map/all_to_all | solution.py:120
  166.9 7.2 %all-to-all-start.5 = ((bf16[16,32,256]{2,1,0:T(8,128)(2,1)}), bf16[16,32,256]{2,1,0:T(8,128)(2,1)S(1)}, u32[]{:S(2)}, u32[]{:S(2)}) async-start(bf16[16,32,256]{2,1,0:T(8,128)(2,1)} %get-tuple-element.12), calls=%async_computation.5 | async-start | bytes 524288 | tf_op jit(solution)/shard_map/all_to_all | solution.py:120
  174.3 1.6 slice.46
  175.9 2.0 reduce
  178.7 13.3 %all-to-all-done.5.returned = bf16[16,32,256]{2,1,0:T(8,128)(2,1)S(1)} async-done(((bf16[16,32,256]{2,1,0:T(8,128)(2,1)}), bf16[16,32,256]{2,1,0:T(8,128)(2,1)S(1)}, u32[]{:S(2)}, u32[]{:S(2)}) %all-to-all-start.5) | async-done | bytes 262176 | tf_op jit(solution)/shard_map/all_to_all | solution.py:120
  192.0 6.0 %all-to-all-start.6 = ((bf16[16,48,128]{2,1,0:T(8,128)(2,1)}), bf16[16,48,128]{2,1,0:T(8,128)(2,1)S(1)}, u32[]{:S(2)}, u32[]{:S(2)}) async-start(bf16[16,48,128]{2,1,0:T(8,128)(2,1)} %pad_maximum_fusion.2), calls=%async_computation.6 | async-start | bytes 393216 | tf_op jit(solution)/shard_map/all_to_all | solution.py:120
  198.0 2.0 collect.1
  200.1 13.4 %all-to-all-done.6 = bf16[16,48,128]{2,1,0:T(8,128)(2,1)S(1)} async-done(((bf16[16,48,128]{2,1,0:T(8,128)(2,1)}), bf16[16,48,128]{2,1,0:T(8,128)(2,1)S(1)}, u32[]{:S(2)}, u32[]{:S(2)}) %all-to-all-start.6) | async-done | bytes 196640 | tf_op jit(solution)/shard_map/all_to_all | solution.py:120
  214.3 5.8 %all-to-all-start.7 = ((f32[16,32,128]{2,1,0:T(8,128)}), f32[16,32,128]{2,1,0:T(8,128)S(1)}, u32[]{:S(2)}, u32[]{:S(2)}) async-start(f32[16,32,128]{2,1,0:T(8,128)} %broadcast_in_dim.11), calls=%async_computation.7 | async-start | bytes 524288 | tf_op jit(solution)/shard_map/all_to_all | solution.py:120
  221.4 16.7 %all-to-all-done.7 = f32[16,32,128]{2,1,0:T(8,128)S(1)} async-done(((f32[16,32,128]{2,1,0:T(8,128)}), f32[16,32,128]{2,1,0:T(8,128)S(1)}, u32[]{:S(2)}, u32[]{:S(2)}) %all-to-all-start.7) | async-done | bytes 262176 | tf_op jit(solution)/shard_map/all_to_all | solution.py:120
  (58 shorter events, 11.0 us)
Async XLA Ops:
  0.6 48.0 %copy-start.6 = (bf16[32,4096]{1,0:T(8,128)(2,1)S(1)}, bf16[32,4096]{1,0:T(8,128)(2,1)}, u32[]{:S(2)}) copy-start(bf16[32,4096]{1,0:T(8,128)(2,1)} %param.11) | copy-start | bytes 786436
  3.8 45.0 %copy-start.8 = (bf16[32,1024]{1,0:T(8,128)(2,1)S(1)}, bf16[32,1024]{1,0:T(8,128)(2,1)}, u32[]{:S(2)}) copy-start(bf16[32,1024]{1,0:T(8,128)(2,1)} %param.13) | copy-start | bytes 196612
  3.8 45.0 %copy-start.9 = (bf16[32,1024]{1,0:T(8,128)(2,1)S(1)}, bf16[32,1024]{1,0:T(8,128)(2,1)}, u32[]{:S(2)}) copy-start(bf16[32,1024]{1,0:T(8,128)(2,1)} %param.12) | copy-start | bytes 196612
  3.8 33.3 %all-to-all-start = ((bf16[16,32,256]{2,1,0:T(8,128)(2,1)}), bf16[16,32,256]{2,1,0:T(8,128)(2,1)S(1)}, u32[]{:S(2)}, u32[]{:S(2)}) async-start(bf16[16,32,256]{2,1,0:T(8,128)(2,1)} %outgoing.1), calls=%async_computation | async-start | bytes 524288 | tf_op jit(solution)/shard_map/all_to_all | solution.py:120
  37.0 0.7 copy-start.4
  41.2 18.4 %all-to-all-start.1 = ((bf16[32,32,256]{2,1,0:T(8,128)(2,1)}), bf16[32,32,256]{2,1,0:T(8,128)(2,1)S(1)}, u32[]{:S(2)}, u32[]{:S(2)}) async-start(bf16[32,32,256]{2,1,0:T(8,128)(2,1)} %get-tuple-element.9), calls=%async_computation.1 | async-start | bytes 1048576 | tf_op jit(solution)/shard_map/all_to_all | solution.py:120
  59.6 38.7 %all-to-all-start.2 = ((bf16[32,32,1280]{2,1,0:T(8,128)(2,1)}), bf16[32,32,1280]{2,1,0:T(8,128)(2,1)S(1)}, u32[]{:S(2)}, u32[]{:S(2)}) async-start(bf16[32,32,1280]{2,1,0:T(8,128)(2,1)} %pad_maximum_fusion), calls=%async_computation.2 | async-start | bytes 5242880 | tf_op jit(solution)/shard_map/all_to_all | solution.py:120
  99.0 1.0 copy-start.3
  100.9 4.1 %collective-permute-start = (f32[1024,128]{0,1:T(8,128)}, f32[1024,128]{0,1:T(8,128)}, u32[]{:S(2)}, u32[]{:S(2)}) collective-permute-start(f32[1024,128]{0,1:T(8,128)} %constant_dynamic-slice_fusion), channel_id=1, source_target_pairs={{0,1},{1,0},{2,3},{3,2},{4,5},{5,4},{6,7},{7,6},{8,9},{9,8},{10,11... | collective-permute-start | bytes 1572872 | tf_op jit(solution)/shard_map/ppermute | solution.py:183
  107.4 5.0 %copy-start.5 = (bf16[1024,128]{0,1:T(8,128)(2,1)}, bf16[1024,128]{0,1:T(8,128)(2,1)S(1)}, u32[]{:S(2)}) copy-start(bf16[1024,128]{0,1:T(8,128)(2,1)S(1)} %get-tuple-element.14) | copy-start | bytes 786436
  107.4 3.4 %collective-permute-start.1 = (bf16[1024,128]{0,1:T(8,128)(2,1)S(1)}, bf16[1024,128]{0,1:T(8,128)(2,1)S(1)}, u32[]{:S(2)}, u32[]{:S(2)}) collective-permute-start(bf16[1024,128]{0,1:T(8,128)(2,1)S(1)} %get-tuple-element.14), channel_id=1, source_target_pairs={{0,1},{1,0},{2,3},{3,2},{4,5},{5,4},{6,7},{7,6},{8,9},{9,8},{10,11... | collective-permute-start | bytes 786440 | tf_op jit(solution)/shard_map/ppermute | solution.py:187
  110.8 1.6 copy-start.7
  112.4 15.0 %all-to-all-start.4 = ((bf16[32,32,256]{2,1,0:T(8,128)(2,1)}), bf16[32,32,256]{2,1,0:T(8,128)(2,1)S(1)}, u32[]{:S(2)}, u32[]{:S(2)}) async-start(bf16[32,32,256]{2,1,0:T(8,128)(2,1)} %bitcast.74), calls=%async_computation.4 | async-start | bytes 1048576 | tf_op jit(solution)/shard_map/all_to_all | solution.py:120
  116.3 2.0 copy-start.1
  127.4 0.8 copy-start
  128.2 38.7 %all-to-all-start.3 = ((bf16[32,32,1280]{2,1,0:T(8,128)(2,1)}), bf16[32,32,1280]{2,1,0:T(8,128)(2,1)S(1)}, u32[]{:S(2)}, u32[]{:S(2)}) async-start(bf16[32,32,1280]{2,1,0:T(8,128)(2,1)} %bitcast.59), calls=%async_computation.3 | async-start | bytes 5242880 | tf_op jit(solution)/shard_map/all_to_all | solution.py:120
  166.9 25.1 %all-to-all-start.5 = ((bf16[16,32,256]{2,1,0:T(8,128)(2,1)}), bf16[16,32,256]{2,1,0:T(8,128)(2,1)S(1)}, u32[]{:S(2)}, u32[]{:S(2)}) async-start(bf16[16,32,256]{2,1,0:T(8,128)(2,1)} %get-tuple-element.12), calls=%async_computation.5 | async-start | bytes 524288 | tf_op jit(solution)/shard_map/all_to_all | solution.py:120
  192.0 6.0 %copy-start.2 = (bf16[16,32,256]{2,1,0:T(8,128)(2,1)}, bf16[16,32,256]{2,1,0:T(8,128)(2,1)S(1)}, u32[]{:S(2)}) copy-start(bf16[16,32,256]{2,1,0:T(8,128)(2,1)S(1)} %all-to-all-done.5.returned) | copy-start | bytes 786436
  192.0 21.5 %all-to-all-start.6 = ((bf16[16,48,128]{2,1,0:T(8,128)(2,1)}), bf16[16,48,128]{2,1,0:T(8,128)(2,1)S(1)}, u32[]{:S(2)}, u32[]{:S(2)}) async-start(bf16[16,48,128]{2,1,0:T(8,128)(2,1)} %pad_maximum_fusion.2), calls=%async_computation.6 | async-start | bytes 393216 | tf_op jit(solution)/shard_map/all_to_all | solution.py:120
  214.3 23.8 %all-to-all-start.7 = ((f32[16,32,128]{2,1,0:T(8,128)}), f32[16,32,128]{2,1,0:T(8,128)S(1)}, u32[]{:S(2)}, u32[]{:S(2)}) async-start(f32[16,32,128]{2,1,0:T(8,128)} %broadcast_in_dim.11), calls=%async_computation.7 | async-start | bytes 524288 | tf_op jit(solution)/shard_map/all_to_all | solution.py:120

commit v2 on v1

v2 whole, which is shorter than its diff:
```python
import functools

import jax
import jax.numpy as jnp
from jax import lax
from jax.experimental import pallas as pl
from jax.experimental.pallas import tpu as pltpu
from jax.sharding import PartitionSpec as P

BLK = 128
NBLK = 32
CAP = 2
TMAX = 64
ROWS = 4096
UNROLL = 8

SMEM = pl.BlockSpec(memory_space=pltpu.SMEM)
VMEM = pl.BlockSpec(memory_space=pltpu.VMEM)
PAIRS = [(i, i ^ 1) for i in range(32)]


def lanes(block):
    return pl.ds(pl.multiple_of(block * BLK, BLK), BLK)


def outgoing_kernel(sends, feats, out):
    for part in range(out.shape[0]):
        for place in range(CAP):
            out[part, :, place * BLK : (place + 1) * BLK] = feats[:, lanes(sends[0, part, place])]


def pack_kernel(weight_self, weight_neigh, cotangent, bias, out):
    own, neigh, extra = weight_self[...], weight_neigh[...], bias[...]
    dims = own.shape[1]
    for peer in range(out.shape[0]):
        out[peer, :, :dims] = own if peer % 2 == 0 else neigh
        out[peer, :, dims : dims + BLK] = cotangent[:, peer * BLK : (peer + 1) * BLK]
        out[peer, :, dims + BLK :] = extra


def aggregate_kernel(rows, cols, count, feats, halo, tiles, packed, out, divisor, ext, acc):
    width = feats.shape[0]
    ones = jnp.ones((16, BLK), jnp.bfloat16)
    for block in range(NBLK):
        ext[block, :width] = feats[:, block * BLK : (block + 1) * BLK]
        ext[block, width:] = ones
    for slot in range(halo.shape[0] * CAP):
        part, place = divmod(slot, CAP)
        ext[NBLK + slot, :width] = halo[part, :, place * BLK : (place + 1) * BLK]
        ext[NBLK + slot, width:] = ones
    acc[...] = jnp.zeros_like(acc)
    live = count[0]

    def step(group, carry):
        for inner in range(UNROLL):
            slot = group * UNROLL + inner
            alive = slot < live
            source = jnp.where(alive, cols[0, slot], 0)
            target = jnp.where(alive, rows[0, slot], NBLK)
            acc[target] += lax.dot_general(
                ext[source], tiles[slot], (((1,), (1,)), ((), ())), preferred_element_type=jnp.float32
            )
        return carry

    lax.fori_loop(0, (live + UNROLL - 1) // UNROLL, step, 0)
    for block in range(NBLK):
        chip, core = divmod(block, 2)
        span = slice(core * BLK, (core + 1) * BLK)
        div = jnp.maximum(acc[block, width : width + 1], 1.0)
        divisor[block : block + 1] = div
        out[2 * chip, :, span] = feats[:, block * BLK : (block + 1) * BLK]
        out[2 * chip + 1, :, span] = (acc[block, :width] / div).astype(jnp.bfloat16)


def pre_kernel(core, weight, data, keep, send):
    product = lax.dot_general(
        weight[...], data[...], (((0,), (0,)), ((), ())), preferred_element_type=jnp.float32
    )
    first, second = product[:, :BLK], product[:, BLK:]
    even = core[0] == 0
    keep[...] = jnp.where(even, first, second)
    send[...] = jnp.where(even, second, first)


def slope_kernel(keep, received, side, layer, grad, sums):
    cotangent = side[:, :BLK].astype(jnp.float32)
    bias = jnp.sum(side[:, BLK:].astype(jnp.float32), axis=1, keepdims=True)
    value, slope = gelu_and_slope(keep[...] + received[...] + bias)
    layer[...] = value.astype(jnp.bfloat16)
    rounded = (cotangent * slope).astype(jnp.bfloat16)
    grad[...] = rounded
    total = jnp.sum(rounded.astype(jnp.float32), axis=1, keepdims=True)
    high = total.astype(jnp.bfloat16).astype(jnp.float32)
    middle = (total - high).astype(jnp.bfloat16).astype(jnp.float32)
    low = total - high - middle
    lane = lax.broadcasted_iota(jnp.int32, (total.shape[0], BLK), 1)
    spread = jnp.where(lane == 0, high, jnp.where(lane == 1, middle, jnp.where(lane == 2, low, 0.0)))
    sums[...] = spread.astype(jnp.bfloat16)


def back_kernel(core, weight, data, grad, other, layer, sums, out, both):
    dims = weight.shape[1]

    @pl.when(pl.program_id(0) == 0)
    def _():
        even = core[0] == 0
        both[:, :BLK] = jnp.where(even, grad[...], other[...])
        both[:, BLK:] = jnp.where(even, other[...], grad[...])

    out[:, :dims] = lax.dot_general(
        data[...], both[...], (((1,), (1,)), ((), ())), preferred_element_type=jnp.float32
    ).astype(jnp.bfloat16)
    out[:, dims : dims + BLK] = layer[...]
    out[:, dims + BLK : dims + 2 * BLK] = sums[...]
    out[:, dims + 2 * BLK :] = jnp.dot(
        weight[...], both[...], preferred_element_type=jnp.float32
    ).astype(jnp.bfloat16)


def scatter_kernel(rows, cols, count, joined, divisor, tiles, out, own, scaled, acc):
    width = own.shape[0]
    start = joined.shape[2] - 2 * BLK
    for block in range(NBLK):
        chip, core = divmod(block, 2)
        span = slice(start + core * BLK, start + (core + 1) * BLK)
        scaled[block] = (
            joined[2 * chip + 1, :, span].astype(jnp.float32) / divisor[block : block + 1]
        ).astype(jnp.bfloat16)
        acc[block] = joined[2 * chip, :, span].astype(jnp.float32)
    acc[NBLK:] = jnp.zeros((acc.shape[0] - NBLK, width, BLK), jnp.float32)
    live = count[0]
    spare = acc.shape[0] - 1

    def step(group, carry):
        for inner in range(UNROLL):
            slot = group * UNROLL + inner
            alive = slot < live
            source = jnp.where(alive, rows[0, slot], 0)
            target = jnp.where(alive, cols[0, slot], spare)
            acc[target] += jnp.dot(scaled[source], tiles[slot], preferred_element_type=jnp.float32)
        return carry

    lax.fori_loop(0, (live + UNROLL - 1) // UNROLL, step, 0)
    for block in range(NBLK):
        own[:, block * BLK : (block + 1) * BLK] = acc[block]
    for slot in range(out.shape[0] * CAP):
        part, place = divmod(slot, CAP)
        out[part, :, place * BLK : (place + 1) * BLK] = acc[NBLK + slot].astype(jnp.bfloat16)
    for part in range(out.shape[0]):
        half, place = divmod(part, out.shape[0] // 2)
        span = slice(place * BLK, (place + 1) * BLK)
        total = joined[half, :, span].astype(jnp.float32)
        for chip in range(1, joined.shape[0] // 2):
            total += joined[2 * chip + half, :, span].astype(jnp.float32)
        out[part, :, CAP * BLK :] = total.astype(jnp.bfloat16)


def piece_kernel(terms, extra, out, *, scale):
    total = terms[0].astype(jnp.float32)
    for part in range(1, terms.shape[0]):
        total += terms[part].astype(jnp.float32)
    total = (total * scale).astype(jnp.bfloat16)
    for part in range(out.shape[0]):
        out[part, : total.shape[0]] = total
        out[part, total.shape[0] :] = extra[...]


def collect_kernel(sends, own, returned, out, acc):
    acc[...] = own[...]
    for part in range(returned.shape[0]):
        for place in range(CAP):
            spot = lanes(sends[0, part, place])
            acc[:, spot] += returned[part, :, place * BLK : (place + 1) * BLK].astype(jnp.float32)
    out[...] = acc[...].astype(jnp.bfloat16)


def finish_kernel(chunks, grad_self, grad_neigh):
    width = grad_self.shape[0]
    count = chunks.shape[0] // 2
    for place in range(count):
        span = slice(place * BLK, (place + 1) * BLK)
        grad_self[:, span] = chunks[place, :width].astype(jnp.float32)
        grad_neigh[:, span] = chunks[count + place, :width].astype(jnp.float32)


def whole(*shape):
    return pl.BlockSpec(shape, lambda *_: (0,) * len(shape))


def part_of(shape, *index):
    return pl.BlockSpec(shape, lambda *_: index)


def pieces(values):
    high = lax.reduce_precision(values, 8, 7)
    rest = values - high
    middle = lax.reduce_precision(rest, 8, 7)
    low = rest - middle
    return jnp.stack([high, middle, low], axis=-1).astype(jnp.bfloat16)


def gelu_and_slope(v):
    root = 0.7978845608028654
    t = jnp.tanh(root * (v + 0.044715 * v * v * v))
    value = 0.5 * v * (1.0 + t)
    slope = 0.5 * (1.0 + t) + 0.5 * v * (1.0 - t * t) * (root * (1.0 + 3 * 0.044715 * v * v))
    return value, slope


def swap(values, axis):
    return lax.all_to_all(values, axis, split_axis=0, concat_axis=0, tiled=True)


def per_device(
    node_feats,
    out_cotangent,
    weight_self,
    weight_neigh,
    out_bias,
    send_blocks,
    tile_rows,
    tile_cols,
    tile_count,
    tile_values,
):
    f32, bf16 = jnp.float32, jnp.bfloat16
    width = node_feats.shape[0]
    parts = lax.axis_size("dom")
    shards = lax.axis_size("feat")
    dims = width * shards
    total = dims + 4 * BLK
    core = (lax.axis_index("feat") % 2).astype(jnp.int32).reshape(1)
    tiles = tile_values[0]

    outgoing = pl.pallas_call(
        outgoing_kernel,
        out_shape=jax.ShapeDtypeStruct((parts, width, CAP * BLK), bf16),
        in_specs=[SMEM, VMEM],
        out_specs=VMEM,
        name="outgoing",
    )(send_blocks, node_feats)
    halo = swap(outgoing, "dom")

    bias = jnp.pad(pieces(out_bias), ((0, 0), (0, BLK - 3)))
    packed = pl.pallas_call(
        pack_kernel,
        out_shape=jax.ShapeDtypeStruct((shards, width, total), bf16),
        grid=(1,),
        in_specs=[whole(width, dims), whole(width, dims), whole(width, ROWS), whole(width, BLK)],
        out_specs=part_of((shards, width, dims + 2 * BLK), 0, 0, 0),
        name="pack",
    )(weight_self, weight_neigh, out_cotangent, bias)

    packed, divisor = pl.pallas_call(
        aggregate_kernel,
        out_shape=(
            jax.ShapeDtypeStruct((shards, width, total), bf16),
            jax.ShapeDtypeStruct((NBLK, BLK), f32),
        ),
        grid=(1,),
        in_specs=[
            SMEM,
            SMEM,
            SMEM,
            whole(width, ROWS),
            whole(parts, width, CAP * BLK),
            whole(TMAX, BLK, BLK),
            pl.BlockSpec(memory_space=pl.ANY),
        ],
        out_specs=(part_of((shards, width, 2 * BLK), 0, 0, dims // (2 * BLK) + 1), whole(NBLK, BLK)),
        scratch_shapes=[
            pltpu.VMEM((NBLK + parts * CAP, width + 16, BLK), bf16),
            pltpu.VMEM((NBLK + 1, width + 16, BLK), f32),
        ],
        input_output_aliases={6: 0},
        name="aggregate",
    )(tile_rows, tile_cols, tile_count, node_feats, halo, tiles, packed)
    packed = swap(packed, "feat").reshape(dims, total)

    chunk = 2 * BLK
    last = dims // chunk + 1
    keep, send = pl.pallas_call(
        pre_kernel,
        out_shape=(jax.ShapeDtypeStruct((dims, BLK), f32),) * 2,
        grid=(dims // chunk,),
        in_specs=[
            SMEM,
            pl.BlockSpec((dims, chunk), lambda i: (0, i)),
            part_of((dims, chunk), 0, last),
        ],
        out_specs=(pl.BlockSpec((chunk, BLK), lambda i: (i, 0)),) * 2,
        name="pre",
    )(core, packed, packed)
    received = lax.ppermute(send, "feat", PAIRS)
    layer, grad, sums = pl.pallas_call(
        slope_kernel,
        out_shape=(jax.ShapeDtypeStruct((dims, BLK), bf16),) * 3,
        grid=(1,),
        in_specs=[whole(dims, BLK), whole(dims, BLK), part_of((dims, chunk), 0, last - 1)],
        out_specs=(whole(dims, BLK),) * 3,
        name="slope",
    )(keep, received, packed)
    other = lax.ppermute(grad, "feat", PAIRS)
    joined = pl.pallas_call(
        back_kernel,
        out_shape=jax.ShapeDtypeStruct((dims, total), bf16),
        grid=(dims // chunk,),
        in_specs=[
            SMEM,
            pl.BlockSpec((chunk, dims), lambda i: (i, 0)),
            pl.BlockSpec((chunk, chunk), lambda i: (i, last)),
            whole(dims, BLK),
            whole(dims, BLK),
            pl.BlockSpec((chunk, BLK), lambda i: (i, 0)),
            pl.BlockSpec((chunk, BLK), lambda i: (i, 0)),
        ],
        out_specs=pl.BlockSpec((chunk, total), lambda i: (i, 0)),
        scratch_shapes=[pltpu.VMEM((dims, chunk), bf16)],
        name="back",
    )(core, packed, packed, grad, other, layer, sums)
    joined = swap(joined.reshape(shards, width, total), "feat")

    outgoing, own = pl.pallas_call(
        scatter_kernel,
        out_shape=(
            jax.ShapeDtypeStruct((parts, width, (CAP + 1) * BLK), bf16),
            jax.ShapeDtypeStruct((width, ROWS), f32),
        ),
        grid=(1,),
        in_specs=[
            SMEM,
            SMEM,
            SMEM,
            whole(shards, width, total),
            whole(NBLK, BLK),
            whole(TMAX, BLK, BLK),
        ],
        out_specs=(whole(parts, width, (CAP + 1) * BLK), whole(width, ROWS)),
        scratch_shapes=[
            pltpu.VMEM((NBLK, width, BLK), bf16),
            pltpu.VMEM((NBLK + parts * CAP + 1, width, BLK), f32),
        ],
        name="scatter",
    )(tile_rows, tile_cols, tile_count, joined, divisor, tiles)
    returned = swap(outgoing, "dom")

    layer_out = jnp.transpose(joined[:, :, dims : dims + BLK], (1, 0, 2)).reshape(width, ROWS)
    bias_part = jnp.sum(joined[:, :, dims + BLK : dims + BLK + 3].astype(f32), axis=(0, 2))
    scale = 1.0 / float(ROWS * parts) ** 0.5
    extra = jnp.pad(pieces(bias_part * scale).T, ((0, 13), (0, BLK - width)))
    chunks = pl.pallas_call(
        functools.partial(piece_kernel, scale=scale),
        out_shape=jax.ShapeDtypeStruct((parts, width + 16, BLK), bf16),
        grid=(1,),
        in_specs=[part_of((parts, width, BLK), 0, 0, CAP), whole(16, BLK)],
        out_specs=whole(parts, width + 16, BLK),
        name="piece",
    )(returned, extra)
    chunks = swap(chunks, "dom")
    feats_grad = pl.pallas_call(
        collect_kernel,
        out_shape=jax.ShapeDtypeStruct((width, ROWS), bf16),
        grid=(1,),
        in_specs=[SMEM, whole(width, ROWS), part_of((parts, width, CAP * BLK), 0, 0, 0)],
        out_specs=whole(width, ROWS),
        scratch_shapes=[pltpu.VMEM((width, ROWS), f32)],
        name="collect",
    )(send_blocks, own, returned)
    grad_self, grad_neigh = pl.pallas_call(
        finish_kernel,
        out_shape=(jax.ShapeDtypeStruct((width, dims), f32),) * 2,
        in_specs=[VMEM],
        out_specs=(VMEM, VMEM),
        name="finish",
    )(chunks)
    grad_bias = jnp.sum(chunks[:, width : width + 3, :width].astype(f32), axis=(0, 1))
    return (layer_out, feats_grad, grad_self, grad_neigh, grad_bias)


def solution(mesh):
    in_specs = (
        P("feat", "dom"),
        P("feat", "dom"),
        P("feat", None),
        P("feat", None),
        P("feat"),
        P("dom", None, None),
        P("dom", None),
        P("dom", None),
        P("dom"),
        P("dom", None, None, None),
    )
    out_specs = (P("feat", "dom"), P("feat", "dom"), P("feat", None), P("feat", None), P("feat"))
    return jax.shard_map(
        per_device, mesh=mesh, in_specs=in_specs, out_specs=out_specs, check_vma=False
    )
```

time: 240 us -> 219 us (0.912)
  waiting for transfers between devices: 143 us -> 89.7 us
  blocking collectives: 0 us -> 44.1 us
  Pallas kernels: 10.4 us -> 32.9 us
  starting transfers between devices: 57.8 us -> 38.8 us
  other arithmetic: 8.83 us -> 2.39 us
  matrix products: 4.31 us -> 0 us
  local copies, waits for them, and re-layouts: 13 us -> 9.06 us
    all_to_all x8 -> x4, waiting for transfers between devices: 141 us -> 86 us  [swap(): return lax.all_to_all(values, axis, split_axis=0, concat_axis=0, tiled=True)]
    all_to_all x0 -> x1, blocking collectives: none -> 44.1 us  [swap(): return lax.all_to_all(values, axis, split_axis=0, concat_axis=0, tiled=True)]
    all_to_all x8 -> x4, starting transfers between devices: 53.9 us -> 34.9 us  [swap(): return lax.all_to_all(values, axis, split_axis=0, concat_axis=0, tiled=True)]
    pallas_call x0 -> x6, Pallas kernels: none -> 18.6 us  [the longest x1 5.35 us: per_device(): pl.pallas_call(back_kernel, out_shape=jax.ShapeDtypeStruct((dims, total),...]
    dot_general x3 -> x0, matrix products: 4.31 us -> none  [the longest x1 1.99 us: per_device(): lax.dot_general(data, grads, (((1,), (1,)), ((), ())), preferred_element_...]
    reduce_sum x5 -> x1, other arithmetic: 4.59 us -> 0.57 us  [per_device(): jnp.sum(chunks[:, width:width + 3, :width].astype(f32), axis=(0, 1))]
    concatenate x3 -> x0, other arithmetic: 2.77 us -> none  [the longest x1 1.82 us: per_device(): packed = swap(jnp.concatenate([both, cot, bias], axis=2), 'feat')]
    concatenate x1 -> x0, local copies, waits for them, and re-layouts: 2.72 us -> none  [per_device(): joined = jnp.concatenate([term.astype(bf16), layer, bias_sum], axis=1)]
  transfers between devices with their start and end apart: 10 -> 6, of which waited for: 10 -> 6; matrix products, arithmetic and copies ran while one was open for 6% -> 2% of each run, Pallas kernels for 2% -> 2%
where the time goes in v2:
time: 219 us; the launch traced here: 218 us
  waiting for transfers between devices  89.7 us (41%)
  blocking collectives  44.1 us (20%)
  starting transfers between devices  38.8 us (18%)
  Pallas kernels  32.9 us (15%)
  local copies, waits for them, and re-layouts  9.06 us (4%)
  other arithmetic  2.39 us (1%)
    all_to_all x4, waiting for transfers between devices, swap(): return lax.all_to_all(values, axis, split_axis=0, concat_axis=0, tiled=True)  86 us
    all_to_all x1, blocking collectives, swap(): return lax.all_to_all(values, axis, split_axis=0, concat_axis=0, tiled=True)  44.1 us
    all_to_all x4, starting transfers between devices, swap(): return lax.all_to_all(values, axis, split_axis=0, concat_axis=0, tiled=True)  34.9 us
    unnamed x13, local copies, waits for them, and re-layouts  6.08 us
    pallas_call x1, Pallas kernels, per_device(): pl.pallas_call(back_kernel, out_shape=jax.ShapeDtypeStruct((dims, total),...  5.35 us
    pallas_call x1, Pallas kernels, per_device(): pl.pallas_call(scatter_kernel, out_shape=(jax.ShapeDtypeStruct((parts, wi...  5.27 us
    pallas_call x1, Pallas kernels, per_device(): pl.pallas_call(aggregate_kernel, out_shape=(jax.ShapeDtypeStruct((shards,...  5.22 us
  transfers between devices with their start and end apart: 6, of which 6 were waited for; matrix products, arithmetic and copies ran while one was open for 2% of the time, Pallas kernels for 2%

profile of v2, /device:TPU:32, one launch (start us, length us, event | category | flops | bytes accessed | tf_op | source)
XLA Modules:
  0.0 218.3 jit_solution(17359855978059682031)
XLA Ops:
  0.6 1.4 copy.27.sends
  2.0 1.7 outgoing.1
  3.7 15.2 %all-to-all-start = ((bf16[16,32,256]{2,1,0:T(8,128)(2,1)}), bf16[16,32,256]{2,1,0:T(8,128)(2,1)S(1)}, u32[]{:S(2)}, u32[]{:S(2)}) async-start(bf16[16,32,256]{2,1,0:T(8,128)(2,1)} %outgoing.1), calls=%async_computation | async-start | bytes 524288 | tf_op jit(solution)/shard_map/all_to_all | solution.py:211
  19.6 0.7 fusion
  21.0 2.9 %pack.1.packed = bf16[32,32,1536]{2,1,0:T(8,128)(2,1)} custom-call(bf16[32,1024]{1,0:T(8,128)(2,1)} %weight_self.1, bf16[32,1024]{1,0:T(8,128)(2,1)} %weight_neigh.1, bf16[32,4096]{1,0:T(8,128)(2,1)} %cotangent.1, bf16[32,128]{1,0:T(8,128)(2,1)} %pad.8.bias), custom_call_target="tpu_custom_call" | custom-call | tf_op jit(solution)/shard_map/pack/pallas_call | solution.py:245
  23.8 13.0 %all-to-all-done.halo = bf16[16,32,256]{2,1,0:T(8,128)(2,1)S(1)} async-done(((bf16[16,32,256]{2,1,0:T(8,128)(2,1)}), bf16[16,32,256]{2,1,0:T(8,128)(2,1)S(1)}, u32[]{:S(2)}, u32[]{:S(2)}) %all-to-all-start) | async-done | bytes 262176 | tf_op jit(solution)/shard_map/all_to_all | solution.py:211
  36.8 0.7 copy-done.2
  37.5 5.2 %aggregate.1 = (bf16[32,32,1536]{2,1,0:T(8,128)(2,1)}, f32[32,128]{1,0:T(8,128)}) custom-call(s32[1,64]{1,0:T(1,128)} %rows.3, s32[1,64]{1,0:T(1,128)} %cols.3, s32[1]{0:T(128)S(6)} %copy.34.count, bf16[32,4096]{1,0:T(8,128)(2,1)} %feats.3, bf16[16,32,256]{2,1,0:T(8,128)(2,1)} %copy-done.2, ...), custom_call_target="tpu_custom_call", output_to_operand_aliasing={{0}: (6, {})} | custom-call | tf_op jit(solution)/shard_map/aggregate/pallas_call | solution.py:254
  42.8 7.3 %all-to-all-start.1 = ((bf16[32,32,1536]{2,1,0:T(8,128)(2,1)}), bf16[32,32,1536]{2,1,0:T(8,128)(2,1)S(1)}, u32[]{:S(2)}, u32[]{:S(2)}) async-start(bf16[32,32,1536]{2,1,0:T(8,128)(2,1)} %get-tuple-element.16), calls=%async_computation.1 | async-start | bytes 6291456 | tf_op jit(solution)/shard_map/all_to_all | solution.py:211
  50.1 40.1 %all-to-all-done.1 = bf16[32,32,1536]{2,1,0:T(8,128)(2,1)S(1)} async-done(((bf16[32,32,1536]{2,1,0:T(8,128)(2,1)}), bf16[32,32,1536]{2,1,0:T(8,128)(2,1)S(1)}, u32[]{:S(2)}, u32[]{:S(2)}) %all-to-all-start.1) | async-done | bytes 3145760 | tf_op jit(solution)/shard_map/all_to_all | solution.py:211
  90.3 1.6 copy-done
  91.9 4.4 %pre.1 = (f32[1024,128]{1,0:T(8,128)}, f32[1024,128]{1,0:T(8,128)}) custom-call(s32[1]{0:T(128)} %bitcast.core, bf16[1024,1536]{1,0:T(8,128)(2,1)} %bitcast.25, bf16[1024,1536]{1,0:T(8,128)(2,1)} %bitcast.26), custom_call_target="tpu_custom_call" | custom-call | tf_op jit(solution)/shard_map/pre/pallas_call | solution.py:282
  96.3 1.9 collective-permute-start
  98.2 2.1 collective-permute-done.received
  100.3 0.8 copy-done.4
  101.1 2.8 %slope.1 = (bf16[1024,128]{1,0:T(8,128)(2,1)}, bf16[1024,128]{1,0:T(8,128)(2,1)}, bf16[1024,128]{1,0:T(8,128)(2,1)}) custom-call(f32[1024,128]{1,0:T(8,128)} %get-tuple-element.17.keep, f32[1024,128]{1,0:T(8,128)} %copy-done.4, bf16[1024,1536]{1,0:T(8,128)(2,1)} %bitcast.27), custom_call_target="tpu_custom_call" | custom-call | tf_op jit(solution)/shard_map/slope/pallas_call | solution.py:295
  103.9 2.0 collective-permute-start.1
  105.9 1.6 collective-permute-done.1.other
  107.5 0.7 copy-done.5
  108.2 5.4 %back.1 = bf16[1024,1536]{1,0:T(8,128)(2,1)} custom-call(s32[1]{0:T(128)} %bitcast.core, bf16[1024,1536]{1,0:T(8,128)(2,1)} %bitcast.28, bf16[1024,1536]{1,0:T(8,128)(2,1)} %bitcast.29, bf16[1024,128]{1,0:T(8,128)(2,1)} %get-tuple-element.19.grad, bf16[1024,128]{1,0:T(8,128)(2,1)} %copy-done.5, bf16[1024,128]{1,0:T(8,128)(2,1)} %get-tuple-element.20.layer, ...), custom_call_target="tpu_custom_call" | custom-call | tf_op jit(solution)/shard_map/back/pallas_call | solution.py:304
  113.6 44.1 %all_to_all.25.joined = bf16[32,32,1536]{2,1,0:T(8,128)(2,1)} all-to-all(bf16[32,32,1536]{2,1,0:T(8,128)(2,1)} %bitcast.30), channel_id=1, replica_groups=mesh['dom'=16,'feat'=32] {'feat'}, dimensions={0} | all-to-all | bytes 6291456 | tf_op jit(solution)/shard_map/all_to_all | solution.py:211
  157.6 5.3 %scatter.1 = (bf16[16,32,384]{2,1,0:T(8,128)(2,1)}, f32[32,4096]{1,0:T(8,128)}) custom-call(s32[1,64]{1,0:T(1,128)} %rows.3, s32[1,64]{1,0:T(1,128)} %cols.3, s32[1]{0:T(128)S(6)} %copy.34.count, bf16[32,32,1536]{2,1,0:T(8,128)(2,1)} %all_to_all.25.joined, f32[32,128]{1,0:T(8,128)} %get-tuple-element.22.divisor, bf16[64,128,128]{2,1,0:T(8,128)(2,1)} %bitcast.32), custom_call_target="tpu_custom_call" | custom-call | tf_op jit(solution)/shard_map/scatter/pallas_call | solution.py:323
  162.9 4.3 %all-to-all-start.3 = ((bf16[16,32,384]{2,1,0:T(8,128)(2,1)}), bf16[16,32,384]{2,1,0:T(8,128)(2,1)S(1)}, u32[]{:S(2)}, u32[]{:S(2)}) async-start(bf16[16,32,384]{2,1,0:T(8,128)(2,1)} %get-tuple-element.24), calls=%async_computation.3 | async-start | bytes 786432 | tf_op jit(solution)/shard_map/all_to_all | solution.py:211
  167.2 1.1 convert_reduce_fusion
  169.0 20.5 %all-to-all-done.3.returned.terms = bf16[16,32,384]{2,1,0:T(8,128)(2,1)S(1)} async-done(((bf16[16,32,384]{2,1,0:T(8,128)(2,1)}), bf16[16,32,384]{2,1,0:T(8,128)(2,1)S(1)}, u32[]{:S(2)}, u32[]{:S(2)}) %all-to-all-start.3) | async-done | bytes 393248 | tf_op jit(solution)/shard_map/all_to_all | solution.py:211
  189.5 0.7 copy-done.1
  190.3 1.6 piece.1
  191.9 8.0 %all-to-all-start.4 = ((bf16[16,48,128]{2,1,0:T(8,128)(2,1)}), bf16[16,48,128]{2,1,0:T(8,128)(2,1)S(1)}, u32[]{:S(2)}, u32[]{:S(2)}) async-start(bf16[16,48,128]{2,1,0:T(8,128)(2,1)} %piece.1), calls=%async_computation.4 | async-start | bytes 393216 | tf_op jit(solution)/shard_map/all_to_all | solution.py:211
  199.9 1.7 copy_bitcast_fusion
  201.6 2.0 collect.1
  203.6 12.3 %all-to-all-done.4.chunks = bf16[16,48,128]{2,1,0:T(8,128)(2,1)S(1)} async-done(((bf16[16,48,128]{2,1,0:T(8,128)(2,1)}), bf16[16,48,128]{2,1,0:T(8,128)(2,1)S(1)}, u32[]{:S(2)}, u32[]{:S(2)}) %all-to-all-start.4) | async-done | bytes 196640 | tf_op jit(solution)/shard_map/all_to_all | solution.py:211
  216.7 1.6 finish.1
  (14 shorter events, 2.0 us)
Async XLA Ops:
  3.7 33.1 %all-to-all-start = ((bf16[16,32,256]{2,1,0:T(8,128)(2,1)}), bf16[16,32,256]{2,1,0:T(8,128)(2,1)S(1)}, u32[]{:S(2)}, u32[]{:S(2)}) async-start(bf16[16,32,256]{2,1,0:T(8,128)(2,1)} %outgoing.1), calls=%async_computation | async-start | bytes 524288 | tf_op jit(solution)/shard_map/all_to_all | solution.py:211
  36.8 0.7 copy-start.2
  42.8 47.5 %all-to-all-start.1 = ((bf16[32,32,1536]{2,1,0:T(8,128)(2,1)}), bf16[32,32,1536]{2,1,0:T(8,128)(2,1)S(1)}, u32[]{:S(2)}, u32[]{:S(2)}) async-start(bf16[32,32,1536]{2,1,0:T(8,128)(2,1)} %get-tuple-element.16), calls=%async_computation.1 | async-start | bytes 6291456 | tf_op jit(solution)/shard_map/all_to_all | solution.py:211
  90.3 1.7 copy-start
  96.3 4.0 %collective-permute-start = (f32[1024,128]{1,0:T(8,128)}, f32[1024,128]{1,0:T(8,128)S(1)}, u32[]{:S(2)}, u32[]{:S(2)}) collective-permute-start(f32[1024,128]{1,0:T(8,128)} %get-tuple-element.18), channel_id=1, source_target_pairs={{0,1},{1,0},{2,3},{3,2},{4,5},{5,4},{6,7},{7,6},{8,9},{9,8},{10,11... | collective-permute-start | bytes 1572872 | tf_op jit(solution)/shard_map/ppermute | solution.py:294
  100.3 0.8 copy-start.4
  103.9 3.6 %collective-permute-start.1 = (bf16[1024,128]{1,0:T(8,128)(2,1)}, bf16[1024,128]{1,0:T(8,128)(2,1)S(1)}, u32[]{:S(2)}, u32[]{:S(2)}) collective-permute-start(bf16[1024,128]{1,0:T(8,128)(2,1)} %get-tuple-element.19.grad), channel_id=1, source_target_pairs={{0,1},{1,0},{2,3},{3,2},{4,5},{5,4},{6,7},{7,6},{8,9},{9,8},{10,11... | collective-permute-start | bytes 786440 | tf_op jit(solution)/shard_map/ppermute | solution.py:303
  107.5 0.7 copy-start.5
  162.9 26.6 %all-to-all-start.3 = ((bf16[16,32,384]{2,1,0:T(8,128)(2,1)}), bf16[16,32,384]{2,1,0:T(8,128)(2,1)S(1)}, u32[]{:S(2)}, u32[]{:S(2)}) async-start(bf16[16,32,384]{2,1,0:T(8,128)(2,1)} %get-tuple-element.24), calls=%async_computation.3 | async-start | bytes 786432 | tf_op jit(solution)/shard_map/all_to_all | solution.py:211
  189.5 0.8 copy-start.1
  191.9 24.1 %all-to-all-start.4 = ((bf16[16,48,128]{2,1,0:T(8,128)(2,1)}), bf16[16,48,128]{2,1,0:T(8,128)(2,1)S(1)}, u32[]{:S(2)}, u32[]{:S(2)}) async-start(bf16[16,48,128]{2,1,0:T(8,128)(2,1)} %piece.1), calls=%async_computation.4 | async-start | bytes 393216 | tf_op jit(solution)/shard_map/all_to_all | solution.py:211
  216.0 0.7 copy-start.3

commit v3 on v2

--- a/solution.py
+++ b/solution.py
@@ -15,7 +15,9 @@
 UNROLL = 8
 
 SMEM = pl.BlockSpec(memory_space=pltpu.SMEM)
+HBM = pltpu.MemorySpace.HBM
 VMEM = pl.BlockSpec(memory_space=pltpu.VMEM)
+PARAMS = pltpu.CompilerParams(vmem_limit_bytes=32 << 20)
 PAIRS = [(i, i ^ 1) for i in range(32)]
 
 
@@ -26,7 +28,7 @@
 def outgoing_kernel(sends, feats, out):
     for part in range(out.shape[0]):
         for place in range(CAP):
-            out[part, :, place * BLK : (place + 1) * BLK] = feats[:, lanes(sends[0, part, place])]
+            out[part, :, place * BLK : (place + 1) * BLK] = feats[:, lanes(sends[0, place, part])]
 
 
 def pack_kernel(weight_self, weight_neigh, cotangent, bias, out):
@@ -72,23 +74,32 @@
         out[2 * chip + 1, :, span] = (acc[block, :width] / div).astype(jnp.bfloat16)
 
 
-def pre_kernel(core, weight, data, keep, send):
-    product = lax.dot_general(
-        weight[...], data[...], (((0,), (0,)), ((), ())), preferred_element_type=jnp.float32
-    )
-    first, second = product[:, :BLK], product[:, BLK:]
+def pre_kernel(core, packed, keep, send):
+    dims, chunk = keep.shape[0], 2 * BLK
+    data = packed[:, dims + chunk :]
     even = core[0] == 0
-    keep[...] = jnp.where(even, first, second)
-    send[...] = jnp.where(even, second, first)
-
-
-def slope_kernel(keep, received, side, layer, grad, sums):
-    cotangent = side[:, :BLK].astype(jnp.float32)
-    bias = jnp.sum(side[:, BLK:].astype(jnp.float32), axis=1, keepdims=True)
+    for start in range(0, dims, chunk):
+        product = lax.dot_general(
+            packed[:, start : start + chunk],
+            data,
+            (((0,), (0,)), ((), ())),
+            preferred_element_type=jnp.float32,
+        )
+        first, second = product[:, :BLK], product[:, BLK:]
+        keep[start : start + chunk] = jnp.where(even, first, second)
+        send[start : start + chunk] = jnp.where(even, second, first)
+
+
+def slope_kernel(keep, received, packed, layer, grad, local, sums):
+    dims = keep.shape[0]
+    cotangent = packed[:, dims : dims + BLK].astype(jnp.float32)
+    bias = packed[:, dims + BLK : dims + 2 * BLK].astype(jnp.float32)
+    bias = jnp.sum(bias, axis=1, keepdims=True)
     value, slope = gelu_and_slope(keep[...] + received[...] + bias)
     layer[...] = value.astype(jnp.bfloat16)
     rounded = (cotangent * slope).astype(jnp.bfloat16)
     grad[...] = rounded
+    local[...] = rounded
     total = jnp.sum(rounded.astype(jnp.float32), axis=1, keepdims=True)
     high = total.astype(jnp.bfloat16).astype(jnp.float32)
     middle = (total - high).astype(jnp.bfloat16).astype(jnp.float32)
@@ -98,8 +109,10 @@
     sums[...] = spread.astype(jnp.bfloat16)
 
 
-def back_kernel(core, weight, data, grad, other, layer, sums, out, both):
-    dims = weight.shape[1]
+def back_kernel(core, packed, grad, other, layer, sums, out, both):
+    rows, total = out.shape
+    dims = total - 4 * BLK
+    span = pl.ds(pl.multiple_of(pl.program_id(0) * rows, rows), rows)
 
     @pl.when(pl.program_id(0) == 0)
     def _():
@@ -108,12 +121,15 @@
         both[:, BLK:] = jnp.where(even, other[...], grad[...])
 
     out[:, :dims] = lax.dot_general(
-        data[...], both[...], (((1,), (1,)), ((), ())), preferred_element_type=jnp.float32
+        packed[span, dims + 2 * BLK :],
+        both[...],
+        (((1,), (1,)), ((), ())),
+        preferred_element_type=jnp.float32,
     ).astype(jnp.bfloat16)
-    out[:, dims : dims + BLK] = layer[...]
-    out[:, dims + BLK : dims + 2 * BLK] = sums[...]
+    out[:, dims : dims + BLK] = layer[span]
+    out[:, dims + BLK : dims + 2 * BLK] = sums[span]
     out[:, dims + 2 * BLK :] = jnp.dot(
-        weight[...], both[...], preferred_element_type=jnp.float32
+        packed[span, :dims], both[...], preferred_element_type=jnp.float32
     ).astype(jnp.bfloat16)
 
 
@@ -156,9 +172,9 @@
 
 
 def piece_kernel(terms, extra, out, *, scale):
-    total = terms[0].astype(jnp.float32)
+    total = terms[0, :, CAP * BLK :].astype(jnp.float32)
     for part in range(1, terms.shape[0]):
-        total += terms[part].astype(jnp.float32)
+        total += terms[part, :, CAP * BLK :].astype(jnp.float32)
     total = (total * scale).astype(jnp.bfloat16)
     for part in range(out.shape[0]):
         out[part, : total.shape[0]] = total
@@ -169,7 +185,7 @@
     acc[...] = own[...]
     for part in range(returned.shape[0]):
         for place in range(CAP):
-            spot = lanes(sends[0, part, place])
+            spot = lanes(sends[0, place, part])
             acc[:, spot] += returned[part, :, place * BLK : (place + 1) * BLK].astype(jnp.float32)
     out[...] = acc[...].astype(jnp.bfloat16)
 
@@ -185,6 +201,10 @@
 
 def whole(*shape):
     return pl.BlockSpec(shape, lambda *_: (0,) * len(shape))
+
+
+def near(array):
+    return pltpu.with_memory_space_constraint(array, pltpu.MemorySpace.VMEM)
 
 
 def part_of(shape, *index):
@@ -229,14 +249,16 @@
     shards = lax.axis_size("feat")
     dims = width * shards
     total = dims + 4 * BLK
+    send_blocks = jnp.transpose(send_blocks, (0, 2, 1))
     core = (lax.axis_index("feat") % 2).astype(jnp.int32).reshape(1)
-    tiles = tile_values[0]
+    tiles = near(tile_values[0])
 
     outgoing = pl.pallas_call(
         outgoing_kernel,
         out_shape=jax.ShapeDtypeStruct((parts, width, CAP * BLK), bf16),
         in_specs=[SMEM, VMEM],
         out_specs=VMEM,
+        compiler_params=PARAMS,
         name="outgoing",
     )(send_blocks, node_feats)
     halo = swap(outgoing, "dom")
@@ -244,105 +266,93 @@
     bias = jnp.pad(pieces(out_bias), ((0, 0), (0, BLK - 3)))
     packed = pl.pallas_call(
         pack_kernel,
-        out_shape=jax.ShapeDtypeStruct((shards, width, total), bf16),
+        out_shape=HBM((shards, width, total), bf16),
         grid=(1,),
         in_specs=[whole(width, dims), whole(width, dims), whole(width, ROWS), whole(width, BLK)],
         out_specs=part_of((shards, width, dims + 2 * BLK), 0, 0, 0),
+        compiler_params=PARAMS,
         name="pack",
     )(weight_self, weight_neigh, out_cotangent, bias)
 
     packed, divisor = pl.pallas_call(
         aggregate_kernel,
         out_shape=(
-            jax.ShapeDtypeStruct((shards, width, total), bf16),
-            jax.ShapeDtypeStruct((NBLK, BLK), f32),
+            HBM((shards, width, total), bf16),
+            pltpu.VMEM((NBLK, BLK), f32),
         ),
         grid=(1,),
         in_specs=[
             SMEM,
             SMEM,
             SMEM,
-            whole(width, ROWS),
-            whole(parts, width, CAP * BLK),
-            whole(TMAX, BLK, BLK),
+            VMEM,
+            VMEM,
+            VMEM,
             pl.BlockSpec(memory_space=pl.ANY),
         ],
-        out_specs=(part_of((shards, width, 2 * BLK), 0, 0, dims // (2 * BLK) + 1), whole(NBLK, BLK)),
+        out_specs=(part_of((shards, width, 2 * BLK), 0, 0, dims // (2 * BLK) + 1), VMEM),
         scratch_shapes=[
             pltpu.VMEM((NBLK + parts * CAP, width + 16, BLK), bf16),
             pltpu.VMEM((NBLK + 1, width + 16, BLK), f32),
         ],
         input_output_aliases={6: 0},
+        compiler_params=PARAMS,
         name="aggregate",
-    )(tile_rows, tile_cols, tile_count, node_feats, halo, tiles, packed)
-    packed = swap(packed, "feat").reshape(dims, total)
+    )(tile_rows, tile_cols, tile_count, near(node_feats), near(halo), tiles, packed)
+    packed = near(swap(packed, "feat").reshape(dims, total))
 
     chunk = 2 * BLK
-    last = dims // chunk + 1
     keep, send = pl.pallas_call(
         pre_kernel,
-        out_shape=(jax.ShapeDtypeStruct((dims, BLK), f32),) * 2,
-        grid=(dims // chunk,),
-        in_specs=[
-            SMEM,
-            pl.BlockSpec((dims, chunk), lambda i: (0, i)),
-            part_of((dims, chunk), 0, last),
-        ],
-        out_specs=(pl.BlockSpec((chunk, BLK), lambda i: (i, 0)),) * 2,
+        out_shape=(pltpu.VMEM((dims, BLK), f32), jax.ShapeDtypeStruct((dims, BLK), f32)),
+        in_specs=[SMEM, VMEM],
+        out_specs=(VMEM, VMEM),
+        compiler_params=PARAMS,
         name="pre",
-    )(core, packed, packed)
+    )(core, packed)
     received = lax.ppermute(send, "feat", PAIRS)
-    layer, grad, sums = pl.pallas_call(
+    layer, grad, local, sums = pl.pallas_call(
         slope_kernel,
-        out_shape=(jax.ShapeDtypeStruct((dims, BLK), bf16),) * 3,
-        grid=(1,),
-        in_specs=[whole(dims, BLK), whole(dims, BLK), part_of((dims, chunk), 0, last - 1)],
-        out_specs=(whole(dims, BLK),) * 3,
+        out_shape=(
+            pltpu.VMEM((dims, BLK), bf16),
+            jax.ShapeDtypeStruct((dims, BLK), bf16),
+            pltpu.VMEM((dims, BLK), bf16),
+            pltpu.VMEM((dims, BLK), bf16),
+        ),
+        in_specs=[VMEM, VMEM, VMEM],
+        out_specs=(VMEM,) * 4,
+        compiler_params=PARAMS,
         name="slope",
-    )(keep, received, packed)
+    )(near(keep), near(received), packed)
     other = lax.ppermute(grad, "feat", PAIRS)
     joined = pl.pallas_call(
         back_kernel,
         out_shape=jax.ShapeDtypeStruct((dims, total), bf16),
         grid=(dims // chunk,),
-        in_specs=[
-            SMEM,
-            pl.BlockSpec((chunk, dims), lambda i: (i, 0)),
-            pl.BlockSpec((chunk, chunk), lambda i: (i, last)),
-            whole(dims, BLK),
-            whole(dims, BLK),
-            pl.BlockSpec((chunk, BLK), lambda i: (i, 0)),
-            pl.BlockSpec((chunk, BLK), lambda i: (i, 0)),
-        ],
+        in_specs=[SMEM, VMEM, VMEM, VMEM, VMEM, VMEM],
         out_specs=pl.BlockSpec((chunk, total), lambda i: (i, 0)),
         scratch_shapes=[pltpu.VMEM((dims, chunk), bf16)],
+        compiler_params=PARAMS,
         name="back",
-    )(core, packed, packed, grad, other, layer, sums)
+    )(core, packed, near(local), near(other), near(layer), near(sums))
     joined = swap(joined.reshape(shards, width, total), "feat")
 
     outgoing, own = pl.pallas_call(
         scatter_kernel,
         out_shape=(
-            jax.ShapeDtypeStruct((parts, width, (CAP + 1) * BLK), bf16),
-            jax.ShapeDtypeStruct((width, ROWS), f32),
+            HBM((parts, width, (CAP + 1) * BLK), bf16),
+            pltpu.VMEM((width, ROWS), f32),
         ),
-        grid=(1,),
-        in_specs=[
-            SMEM,
-            SMEM,
-            SMEM,
-            whole(shards, width, total),
-            whole(NBLK, BLK),
-            whole(TMAX, BLK, BLK),
-        ],
-        out_specs=(whole(parts, width, (CAP + 1) * BLK), whole(width, ROWS)),
+        in_specs=[SMEM, SMEM, SMEM, VMEM, VMEM, VMEM],
+        out_specs=(VMEM, VMEM),
         scratch_shapes=[
             pltpu.VMEM((NBLK, width, BLK), bf16),
             pltpu.VMEM((NBLK + parts * CAP + 1, width, BLK), f32),
         ],
+        compiler_params=PARAMS,
         name="scatter",
-    )(tile_rows, tile_cols, tile_count, joined, divisor, tiles)
-    returned = swap(outgoing, "dom")
+    )(tile_rows, tile_cols, tile_count, near(joined), near(divisor), tiles)
+    returned = near(swap(outgoing, "dom"))
 
     layer_out = jnp.transpose(joined[:, :, dims : dims + BLK], (1, 0, 2)).reshape(width, ROWS)
     bias_part = jnp.sum(joined[:, :, dims + BLK : dims + BLK + 3].astype(f32), axis=(0, 2))
@@ -350,29 +360,30 @@
     extra = jnp.pad(pieces(bias_part * scale).T, ((0, 13), (0, BLK - width)))
     chunks = pl.pallas_call(
         functools.partial(piece_kernel, scale=scale),
-        out_shape=jax.ShapeDtypeStruct((parts, width + 16, BLK), bf16),
-        grid=(1,),
-        in_specs=[part_of((parts, width, BLK), 0, 0, CAP), whole(16, BLK)],
-        out_specs=whole(parts, width + 16, BLK),
+        out_shape=HBM((parts, width + 16, BLK), bf16),
+        in_specs=[VMEM, VMEM],
+        out_specs=VMEM,
+        compiler_params=PARAMS,
         name="piece",
-    )(returned, extra)
+    )(returned, near(extra))
     chunks = swap(chunks, "dom")
     feats_grad = pl.pallas_call(
         collect_kernel,
         out_shape=jax.ShapeDtypeStruct((width, ROWS), bf16),
-        grid=(1,),
-        in_specs=[SMEM, whole(width, ROWS), part_of((parts, width, CAP * BLK), 0, 0, 0)],
-        out_specs=whole(width, ROWS),
+        in_specs=[SMEM, VMEM, VMEM],
+        out_specs=VMEM,
         scratch_shapes=[pltpu.VMEM((width, ROWS), f32)],
+        compiler_params=PARAMS,
         name="collect",
-    )(send_blocks, own, returned)
+    )(send_blocks, near(own), returned)
     grad_self, grad_neigh = pl.pallas_call(
         finish_kernel,
         out_shape=(jax.ShapeDtypeStruct((width, dims), f32),) * 2,
         in_specs=[VMEM],
         out_specs=(VMEM, VMEM),
+        compiler_params=PARAMS,
         name="finish",
-    )(chunks)
+    )(near(chunks))
     grad_bias = jnp.sum(chunks[:, width : width + 3, :width].astype(f32), axis=(0, 1))
     return (layer_out, feats_grad, grad_self, grad_neigh, grad_bias)
 

time: 219 us -> 203 us (0.927)
  Pallas kernels: 32.9 us -> 15.2 us
  starting transfers between devices: 38.8 us -> 42.7 us
    pallas_call x6, Pallas kernels: 22.1 us -> 8.79 us  [the longest x1 2.55 us: per_device(): pl.pallas_call(aggregate_kernel, out_shape=(HBM((shards, width, total), b...]
    all_to_all x4, starting transfers between devices: 34.9 us -> 38.8 us  [swap(): return lax.all_to_all(values, axis, split_axis=0, concat_axis=0, tiled=True)]
    pallas_call x1, Pallas kernels: 5.35 us -> 2.01 us  [per_device(): pl.pallas_call(back_kernel, out_shape=jax.ShapeDtypeStruct((dims, total),...]
    unnamed x13 -> x26, local copies, waits for them, and re-layouts: 6.08 us -> 6.27 us
  transfers between devices with their start and end apart: 6 -> 6, of which waited for: 6 -> 6; matrix products, arithmetic and copies ran while one was open for 2% -> 1% of each run, Pallas kernels for 2% -> 2%
where the time goes in v3:
time: 203 us; the launch traced here: 202 us
  waiting for transfers between devices  90.4 us (45%)
  blocking collectives  43.2 us (21%)
  starting transfers between devices  42.7 us (21%)
  Pallas kernels  15.2 us (7%)
  local copies, waits for them, and re-layouts  7.13 us (4%)
  other arithmetic  2.17 us (1%)
    all_to_all x4, waiting for transfers between devices, swap(): return lax.all_to_all(values, axis, split_axis=0, concat_axis=0, tiled=True)  87.2 us
    all_to_all x1, blocking collectives, swap(): return lax.all_to_all(values, axis, split_axis=0, concat_axis=0, tiled=True)  43.2 us
    all_to_all x4, starting transfers between devices, swap(): return lax.all_to_all(values, axis, split_axis=0, concat_axis=0, tiled=True)  38.8 us
    unnamed x26, local copies, waits for them, and re-layouts  6.27 us
  transfers between devices with their start and end apart: 6, of which 6 were waited for; matrix products, arithmetic and copies ran while one was open for 1% of the time, Pallas kernels for 2%

profile of v3, /device:TPU:32, one launch (start us, length us, event | category | flops | bytes accessed | tf_op | source)
XLA Modules:
  0.0 202.3 jit_solution(10196328305506752267)
XLA Ops:
  0.7 1.1 copy-done.2
  1.7 0.7 copy-done.9
  2.4 1.3 outgoing.1
  3.7 15.2 %all-to-all-start = ((bf16[16,32,256]{2,1,0:T(8,128)(2,1)}), bf16[16,32,256]{2,1,0:T(8,128)(2,1)S(1)}, u32[]{:S(2)}, u32[]{:S(2)}) async-start(bf16[16,32,256]{2,1,0:T(8,128)(2,1)} %outgoing.1), calls=%async_computation | async-start | bytes 524288 | tf_op jit(solution)/shard_map/all_to_all | solution.py:231
  19.6 0.7 fusion
  20.4 0.9 copy-done.6
  21.4 0.8 copy-done.7
  22.2 0.8 copy-done.8
  23.0 1.8 pack.1.packed
  24.9 12.0 %all-to-all-done.halo = bf16[16,32,256]{2,1,0:T(8,128)(2,1)S(1)} async-done(((bf16[16,32,256]{2,1,0:T(8,128)(2,1)}), bf16[16,32,256]{2,1,0:T(8,128)(2,1)S(1)}, u32[]{:S(2)}, u32[]{:S(2)}) %all-to-all-start) | async-done | bytes 262176 | tf_op jit(solution)/shard_map/all_to_all | solution.py:231
  36.9 2.5 %aggregate.1 = (bf16[32,32,1536]{2,1,0:T(8,128)(2,1)}, f32[32,128]{1,0:T(8,128)S(1)}) custom-call(s32[1,64]{1,0:T(1,128)S(1)} %copy-done.11, s32[1,64]{1,0:T(1,128)S(1)} %copy-done.12, s32[1]{0:T(128)S(6)} %copy.28.count, bf16[32,4096]{1,0:T(8,128)(2,1)S(1)} %copy-done.3, ...), custom_call_target="tpu_custom_call", output_to_operand_aliasing={{0}: (6, {})} | custom-call | tf_op jit(solution)/shard_map/aggregate/pallas_call | solution.py:277
  39.4 7.3 %all-to-all-start.1 = ((bf16[32,32,1536]{2,1,0:T(8,128)(2,1)}), bf16[32,32,1536]{2,1,0:T(8,128)(2,1)S(1)}, u32[]{:S(2)}, u32[]{:S(2)}) async-start(bf16[32,32,1536]{2,1,0:T(8,128)(2,1)} %get-tuple-element.17), calls=%async_computation.1 | async-start | bytes 6291456 | tf_op jit(solution)/shard_map/all_to_all | solution.py:231
  46.8 40.1 %all-to-all-done.1 = bf16[32,32,1536]{2,1,0:T(8,128)(2,1)S(1)} async-done(((bf16[32,32,1536]{2,1,0:T(8,128)(2,1)}), bf16[32,32,1536]{2,1,0:T(8,128)(2,1)S(1)}, u32[]{:S(2)}, u32[]{:S(2)}) %all-to-all-start.1) | async-done | bytes 3145760 | tf_op jit(solution)/shard_map/all_to_all | solution.py:231
  86.9 0.8 pre.1
  87.7 1.9 collective-permute-start
  89.6 1.9 collective-permute-done.received
  92.2 2.0 %collective-permute-start.1 = (bf16[1024,128]{1,0:T(8,128)(2,1)S(1)}, bf16[1024,128]{1,0:T(8,128)(2,1)S(1)}, u32[]{:S(2)}, u32[]{:S(2)}) collective-permute-start(bf16[1024,128]{1,0:T(8,128)(2,1)S(1)} %get-tuple-element.21), channel_id=1, source_target_pairs={{0,1},{1,0},{2,3},{3,2},{4,5},{5,4},{6,7},{7,6},{8,9},{9,8},{10,11... | collective-permute-start | bytes 786440 | tf_op jit(solution)/shard_map/ppermute | solution.py:327
  94.2 1.4 collective-permute-done.1.other
  95.6 2.0 back.1
  97.6 43.2 %all_to_all.25.joined = bf16[32,32,1536]{2,1,0:T(8,128)(2,1)S(1)} all-to-all(bf16[32,32,1536]{2,1,0:T(8,128)(2,1)S(1)} %bitcast.29), channel_id=1, replica_groups=mesh['dom'=16,'feat'=32] {'feat'}, dimensions={0} | all-to-all | bytes 6291456 | tf_op jit(solution)/shard_map/all_to_all | solution.py:231
  140.8 2.3 %scatter.1 = (bf16[16,32,384]{2,1,0:T(8,128)(2,1)}, f32[32,4096]{1,0:T(8,128)S(1)}) custom-call(s32[1,64]{1,0:T(1,128)S(1)} %copy-done.11, s32[1,64]{1,0:T(1,128)S(1)} %copy-done.12, s32[1]{0:T(128)S(6)} %copy.28.count, bf16[32,32,1536]{2,1,0:T(8,128)(2,1)S(1)} %all_to_all.25.joined, f32[32,128]{1,0:T(8,128)S(1)} %get-tuple-element.24.divisor, ...), custom_call_target="tpu_custom_call" | custom-call | tf_op jit(solution)/shard_map/scatter/pallas_call | solution.py:340
  143.1 0.8 copy-done.4
  143.9 8.2 %all-to-all-start.3 = ((bf16[16,32,384]{2,1,0:T(8,128)(2,1)}), bf16[16,32,384]{2,1,0:T(8,128)(2,1)S(1)}, u32[]{:S(2)}, u32[]{:S(2)}) async-start(bf16[16,32,384]{2,1,0:T(8,128)(2,1)} %get-tuple-element.26), calls=%async_computation.3 | async-start | bytes 786432 | tf_op jit(solution)/shard_map/all_to_all | solution.py:231
  152.3 22.1 %all-to-all-done.3.returned.terms = bf16[16,32,384]{2,1,0:T(8,128)(2,1)S(1)} async-done(((bf16[16,32,384]{2,1,0:T(8,128)(2,1)}), bf16[16,32,384]{2,1,0:T(8,128)(2,1)S(1)}, u32[]{:S(2)}, u32[]{:S(2)}) %all-to-all-start.3) | async-done | bytes 393248 | tf_op jit(solution)/shard_map/all_to_all | solution.py:231
  174.4 0.7 piece.1
  175.1 8.0 %all-to-all-start.4 = ((bf16[16,48,128]{2,1,0:T(8,128)(2,1)}), bf16[16,48,128]{2,1,0:T(8,128)(2,1)}, u32[]{:S(2)}, u32[]{:S(2)}) async-start(bf16[16,48,128]{2,1,0:T(8,128)(2,1)} %piece.1), calls=%async_computation.4 | async-start | bytes 393216 | tf_op jit(solution)/shard_map/all_to_all | solution.py:231
  183.2 0.7 copy_bitcast_fusion
  183.9 1.0 copy-done.5
  184.9 1.5 collect.1
  186.4 12.9 %all-to-all-done.4.chunks = bf16[16,48,128]{2,1,0:T(8,128)(2,1)} async-done(((bf16[16,48,128]{2,1,0:T(8,128)(2,1)}), bf16[16,48,128]{2,1,0:T(8,128)(2,1)}, u32[]{:S(2)}, u32[]{:S(2)}) %all-to-all-start.4) | async-done | bytes 196640 | tf_op jit(solution)/shard_map/all_to_all | solution.py:231
  199.3 1.3 convert_reduce_fusion.1
  200.6 1.6 finish.1
  (27 shorter events, 1.0 us)
Async XLA Ops:
  0.6 36.2 %copy-start = (bf16[1,64,128,128]{3,2,1,0:T(8,128)(2,1)S(1)}, bf16[1,64,128,128]{3,2,1,0:T(8,128)(2,1)}, u32[]{:S(2)}) copy-start(bf16[1,64,128,128]{3,2,1,0:T(8,128)(2,1)} %param.19) | copy-start | bytes 6291460
  0.6 1.1 copy-start.2
  1.7 0.7 copy-start.9
  2.4 34.5 %copy-start.3 = (bf16[32,4096]{1,0:T(8,128)(2,1)S(1)}, bf16[32,4096]{1,0:T(8,128)(2,1)}, u32[]{:S(2)}) copy-start(bf16[32,4096]{1,0:T(8,128)(2,1)} %feats.3) | copy-start | bytes 786436
  3.7 33.1 %all-to-all-start = ((bf16[16,32,256]{2,1,0:T(8,128)(2,1)}), bf16[16,32,256]{2,1,0:T(8,128)(2,1)S(1)}, u32[]{:S(2)}, u32[]{:S(2)}) async-start(bf16[16,32,256]{2,1,0:T(8,128)(2,1)} %outgoing.1), calls=%async_computation | async-start | bytes 524288 | tf_op jit(solution)/shard_map/all_to_all | solution.py:231
  20.4 1.0 copy-start.6
  21.4 0.8 copy-start.7
  22.2 0.8 copy-start.8
  23.0 13.8 %copy-start.11 = (s32[1,64]{1,0:T(1,128)S(1)}, s32[1,64]{1,0:T(1,128)}, u32[]{:S(2)}) copy-start(s32[1,64]{1,0:T(1,128)} %rows.3) | copy-start | bytes 772
  23.0 13.8 %copy-start.12 = (s32[1,64]{1,0:T(1,128)S(1)}, s32[1,64]{1,0:T(1,128)}, u32[]{:S(2)}) copy-start(s32[1,64]{1,0:T(1,128)} %cols.3) | copy-start | bytes 772
  39.4 47.5 %all-to-all-start.1 = ((bf16[32,32,1536]{2,1,0:T(8,128)(2,1)}), bf16[32,32,1536]{2,1,0:T(8,128)(2,1)S(1)}, u32[]{:S(2)}, u32[]{:S(2)}) async-start(bf16[32,32,1536]{2,1,0:T(8,128)(2,1)} %get-tuple-element.17), calls=%async_computation.1 | async-start | bytes 6291456 | tf_op jit(solution)/shard_map/all_to_all | solution.py:231
  87.7 3.8 %collective-permute-start = (f32[1024,128]{1,0:T(8,128)S(1)}, f32[1024,128]{1,0:T(8,128)S(1)}, u32[]{:S(2)}, u32[]{:S(2)}) collective-permute-start(f32[1024,128]{1,0:T(8,128)S(1)} %get-tuple-element.19), channel_id=1, source_target_pairs={{0,1},{1,0},{2,3},{3,2},{4,5},{5,4},{6,7},{7,6},{8,9},{9,8},{10,11... | collective-permute-start | bytes 1572872 | tf_op jit(solution)/shard_map/ppermute | solution.py:313
  92.2 3.4 %collective-permute-start.1 = (bf16[1024,128]{1,0:T(8,128)(2,1)S(1)}, bf16[1024,128]{1,0:T(8,128)(2,1)S(1)}, u32[]{:S(2)}, u32[]{:S(2)}) collective-permute-start(bf16[1024,128]{1,0:T(8,128)(2,1)S(1)} %get-tuple-element.21), channel_id=1, source_target_pairs={{0,1},{1,0},{2,3},{3,2},{4,5},{5,4},{6,7},{7,6},{8,9},{9,8},{10,11... | collective-permute-start | bytes 786440 | tf_op jit(solution)/shard_map/ppermute | solution.py:327
  97.6 43.2 %copy-start.1 = (bf16[1,64,128,128]{3,2,1,0:T(8,128)(2,1)S(1)}, bf16[1,64,128,128]{3,2,1,0:T(8,128)(2,1)}, u32[]{:S(2)}) copy-start(bf16[1,64,128,128]{3,2,1,0:T(8,128)(2,1)} %param.19) | copy-start | bytes 6291460
  140.8 43.1 %copy-start.10 = (s32[1,16,2]{1,2,0:T(2,128)S(1)}, s32[1,16,2]{1,2,0:T(2,128)}, u32[]{:S(2)}) copy-start(s32[1,16,2]{1,2,0:T(2,128)} %param.15) | copy-start | bytes 388
  143.1 0.8 copy-start.4
  143.9 30.5 %all-to-all-start.3 = ((bf16[16,32,384]{2,1,0:T(8,128)(2,1)}), bf16[16,32,384]{2,1,0:T(8,128)(2,1)S(1)}, u32[]{:S(2)}, u32[]{:S(2)}) async-start(bf16[16,32,384]{2,1,0:T(8,128)(2,1)} %get-tuple-element.26), calls=%async_computation.3 | async-start | bytes 786432 | tf_op jit(solution)/shard_map/all_to_all | solution.py:231
  175.1 24.2 %all-to-all-start.4 = ((bf16[16,48,128]{2,1,0:T(8,128)(2,1)}), bf16[16,48,128]{2,1,0:T(8,128)(2,1)}, u32[]{:S(2)}, u32[]{:S(2)}) async-start(bf16[16,48,128]{2,1,0:T(8,128)(2,1)} %piece.1), calls=%async_computation.4 | async-start | bytes 393216 | tf_op jit(solution)/shard_map/all_to_all | solution.py:231
  183.9 1.0 copy-start.5

commit v4 on v3

--- a/solution.py
+++ b/solution.py
@@ -31,13 +31,40 @@
             out[part, :, place * BLK : (place + 1) * BLK] = feats[:, lanes(sends[0, place, part])]
 
 
+SIDE = 8 * 32
+TAIL = 9 * 32
+HEIGHT = TAIL + 16
+
+
+def interleave():
+    lane = lax.broadcasted_iota(jnp.int32, (2 * BLK, 2 * BLK), 0)
+    spot = lax.broadcasted_iota(jnp.int32, (2 * BLK, 2 * BLK), 1)
+    goal = (lane % 32) // 16 * BLK + lane // 32 * 16 + lane % 16
+    return jnp.where(goal == spot, 1.0, 0.0).astype(jnp.bfloat16)
+
+
 def pack_kernel(weight_self, weight_neigh, cotangent, bias, out):
-    own, neigh, extra = weight_self[...], weight_neigh[...], bias[...]
-    dims = own.shape[1]
+    order = interleave()
+    for path, weight in enumerate((weight_self, weight_neigh)):
+        for block in range(weight.shape[1] // (2 * BLK)):
+            mixed = jnp.dot(
+                weight[:, 2 * block * BLK : 2 * (block + 1) * BLK],
+                order,
+                preferred_element_type=jnp.float32,
+            ).astype(jnp.bfloat16)
+            for half in range(2):
+                part = mixed[:, half * BLK : (half + 1) * BLK]
+                for group in range(out.shape[0] // 4):
+                    out[4 * group + 2 * half + path, block * 32 : (block + 1) * 32] = part
     for peer in range(out.shape[0]):
-        out[peer, :, :dims] = own if peer % 2 == 0 else neigh
-        out[peer, :, dims : dims + BLK] = cotangent[:, peer * BLK : (peer + 1) * BLK]
-        out[peer, :, dims + BLK :] = extra
+        half = peer // 2 % 2
+        first = 4 * (peer // 4) + 2 * (peer % 2)
+        rows = slice(half * 16, (half + 1) * 16)
+        for place in range(2):
+            out[peer, SIDE + 16 * place : SIDE + 16 * (place + 1)] = cotangent[
+                rows, (first + place) * BLK : (first + place + 1) * BLK
+            ]
+        out[peer, TAIL:] = bias[rows]
 
 
 def aggregate_kernel(rows, cols, count, feats, halo, tiles, packed, out, divisor, ext, acc):
@@ -66,83 +93,92 @@
 
     lax.fori_loop(0, (live + UNROLL - 1) // UNROLL, step, 0)
     for block in range(NBLK):
-        chip, core = divmod(block, 2)
-        span = slice(core * BLK, (core + 1) * BLK)
+        group, place = divmod(block, 4)
+        span = slice(place * 32, (place + 1) * 32)
         div = jnp.maximum(acc[block, width : width + 1], 1.0)
         divisor[block : block + 1] = div
-        out[2 * chip, :, span] = feats[:, block * BLK : (block + 1) * BLK]
-        out[2 * chip + 1, :, span] = (acc[block, :width] / div).astype(jnp.bfloat16)
-
-
-def pre_kernel(core, packed, keep, send):
-    dims, chunk = keep.shape[0], 2 * BLK
-    data = packed[:, dims + chunk :]
+        mean = (acc[block, :width] / div).astype(jnp.bfloat16)
+        for half in range(2):
+            out[4 * group + 2 * half, span] = feats[:, block * BLK : (block + 1) * BLK]
+            out[4 * group + 2 * half + 1, span] = mean
+
+
+def pre_kernel(core, packed, weight, data, keep, send):
+    dims, outs = weight.shape
+    for block in range(4):
+        span = slice(block * BLK, (block + 1) * BLK)
+        weight[:, span] = packed[:, block * 32 : (block + 1) * 32].reshape(dims, BLK)
+        data[:, span] = packed[:, (4 + block) * 32 : (5 + block) * 32].reshape(dims, BLK)
     even = core[0] == 0
-    for start in range(0, dims, chunk):
+    for start in range(0, outs, 2 * BLK):
+        rows = slice(start, start + 2 * BLK)
         product = lax.dot_general(
-            packed[:, start : start + chunk],
-            data,
-            (((0,), (0,)), ((), ())),
-            preferred_element_type=jnp.float32,
+            weight[:, rows], data[...], (((0,), (0,)), ((), ())), preferred_element_type=jnp.float32
         )
-        first, second = product[:, :BLK], product[:, BLK:]
-        keep[start : start + chunk] = jnp.where(even, first, second)
-        send[start : start + chunk] = jnp.where(even, second, first)
+        first, second = product[:, : 2 * BLK], product[:, 2 * BLK :]
+        keep[rows] = jnp.where(even, first, second)
+        send[rows] = jnp.where(even, second, first)
 
 
 def slope_kernel(keep, received, packed, layer, grad, local, sums):
-    dims = keep.shape[0]
-    cotangent = packed[:, dims : dims + BLK].astype(jnp.float32)
-    bias = packed[:, dims + BLK : dims + 2 * BLK].astype(jnp.float32)
+    outs = keep.shape[0]
+    bias = packed[:, TAIL:].reshape(outs, BLK).astype(jnp.float32)
     bias = jnp.sum(bias, axis=1, keepdims=True)
-    value, slope = gelu_and_slope(keep[...] + received[...] + bias)
-    layer[...] = value.astype(jnp.bfloat16)
-    rounded = (cotangent * slope).astype(jnp.bfloat16)
-    grad[...] = rounded
-    local[...] = rounded
-    total = jnp.sum(rounded.astype(jnp.float32), axis=1, keepdims=True)
+    total = jnp.zeros((outs, 1), jnp.float32)
+    for place in range(2):
+        span = slice(place * BLK, (place + 1) * BLK)
+        cotangent = packed[:, SIDE + 16 * place : SIDE + 16 * (place + 1)].reshape(outs, BLK)
+        value, slope = gelu_and_slope(keep[:, span] + received[:, span] + bias)
+        layer[:, span] = value.astype(jnp.bfloat16)
+        rounded = (cotangent.astype(jnp.float32) * slope).astype(jnp.bfloat16)
+        grad[:, span] = rounded
+        local[:, span] = rounded
+        total += jnp.sum(rounded.astype(jnp.float32), axis=1, keepdims=True)
     high = total.astype(jnp.bfloat16).astype(jnp.float32)
     middle = (total - high).astype(jnp.bfloat16).astype(jnp.float32)
     low = total - high - middle
-    lane = lax.broadcasted_iota(jnp.int32, (total.shape[0], BLK), 1)
+    lane = lax.broadcasted_iota(jnp.int32, (outs, BLK), 1)
     spread = jnp.where(lane == 0, high, jnp.where(lane == 1, middle, jnp.where(lane == 2, low, 0.0)))
     sums[...] = spread.astype(jnp.bfloat16)
 
 
-def back_kernel(core, packed, grad, other, layer, sums, out, both):
-    rows, total = out.shape
-    dims = total - 4 * BLK
-    span = pl.ds(pl.multiple_of(pl.program_id(0) * rows, rows), rows)
+def back_kernel(core, weight, data, grad, other, layer, sums, out, both):
+    peers = out.shape[0]
+    rows = pl.ds(pl.multiple_of(pl.program_id(0) * peers * 32, peers * 32), peers * 32)
+    outs = pl.ds(pl.multiple_of(pl.program_id(0) * peers * 16, peers * 16), peers * 16)
 
     @pl.when(pl.program_id(0) == 0)
     def _():
         even = core[0] == 0
-        both[:, :BLK] = jnp.where(even, grad[...], other[...])
-        both[:, BLK:] = jnp.where(even, other[...], grad[...])
-
-    out[:, :dims] = lax.dot_general(
-        packed[span, dims + 2 * BLK :],
-        both[...],
-        (((1,), (1,)), ((), ())),
-        preferred_element_type=jnp.float32,
+        both[:, : 2 * BLK] = jnp.where(even, grad[...], other[...])
+        both[:, 2 * BLK :] = jnp.where(even, other[...], grad[...])
+
+    term = lax.dot_general(
+        data[rows], both[...], (((1,), (1,)), ((), ())), preferred_element_type=jnp.float32
     ).astype(jnp.bfloat16)
-    out[:, dims : dims + BLK] = layer[span]
-    out[:, dims + BLK : dims + 2 * BLK] = sums[span]
-    out[:, dims + 2 * BLK :] = jnp.dot(
-        packed[span, :dims], both[...], preferred_element_type=jnp.float32
-    ).astype(jnp.bfloat16)
+    back = jnp.dot(weight[rows], both[...], preferred_element_type=jnp.float32).astype(jnp.bfloat16)
+    for block in range(4):
+        span = slice(block * BLK, (block + 1) * BLK)
+        out[:, block * 32 : (block + 1) * 32] = term[:, span].reshape(peers, 32, BLK)
+        out[:, (4 + block) * 32 : (5 + block) * 32] = back[:, span].reshape(peers, 32, BLK)
+    for place in range(2):
+        value = layer[outs, place * BLK : (place + 1) * BLK]
+        out[:, SIDE + 16 * place : SIDE + 16 * (place + 1)] = value.reshape(peers, 16, BLK)
+    out[:, TAIL:] = sums[outs].reshape(peers, 16, BLK)
 
 
 def scatter_kernel(rows, cols, count, joined, divisor, tiles, out, own, scaled, acc):
     width = own.shape[0]
-    start = joined.shape[2] - 2 * BLK
     for block in range(NBLK):
-        chip, core = divmod(block, 2)
-        span = slice(start + core * BLK, start + (core + 1) * BLK)
-        scaled[block] = (
-            joined[2 * chip + 1, :, span].astype(jnp.float32) / divisor[block : block + 1]
-        ).astype(jnp.bfloat16)
-        acc[block] = joined[2 * chip, :, span].astype(jnp.float32)
+        group, place = divmod(block, 4)
+        span = slice((4 + place) * 32, (5 + place) * 32)
+        own_path, neigh_path = (
+            joined[4 * group + path, span].astype(jnp.float32)
+            + joined[4 * group + 2 + path, span].astype(jnp.float32)
+            for path in range(2)
+        )
+        scaled[block] = (neigh_path / divisor[block : block + 1]).astype(jnp.bfloat16)
+        acc[block] = own_path
     acc[NBLK:] = jnp.zeros((acc.shape[0] - NBLK, width, BLK), jnp.float32)
     live = count[0]
     spare = acc.shape[0] - 1
@@ -163,12 +199,22 @@
         part, place = divmod(slot, CAP)
         out[part, :, place * BLK : (place + 1) * BLK] = acc[NBLK + slot].astype(jnp.bfloat16)
     for part in range(out.shape[0]):
-        half, place = divmod(part, out.shape[0] // 2)
-        span = slice(place * BLK, (place + 1) * BLK)
-        total = joined[half, :, span].astype(jnp.float32)
-        for chip in range(1, joined.shape[0] // 2):
-            total += joined[2 * chip + half, :, span].astype(jnp.float32)
+        path, half, place = part // 8, part // 4 % 2, part % 4
+        span = slice(place * 32, (place + 1) * 32)
+        total = joined[2 * half + path, span].astype(jnp.float32)
+        for group in range(1, joined.shape[0] // 4):
+            total += joined[4 * group + 2 * half + path, span].astype(jnp.float32)
         out[part, :, CAP * BLK :] = total.astype(jnp.bfloat16)
+
+
+def layer_kernel(joined, out):
+    for peer in range(joined.shape[0]):
+        half = peer // 2 % 2
+        first = 4 * (peer // 4) + 2 * (peer % 2)
+        for place in range(2):
+            out[half * 16 : (half + 1) * 16, (first + place) * BLK : (first + place + 1) * BLK] = (
+                joined[peer, SIDE + 16 * place : SIDE + 16 * (place + 1)]
+            )
 
 
 def piece_kernel(terms, extra, out, *, scale):
@@ -192,11 +238,15 @@
 
 def finish_kernel(chunks, grad_self, grad_neigh):
     width = grad_self.shape[0]
-    count = chunks.shape[0] // 2
-    for place in range(count):
-        span = slice(place * BLK, (place + 1) * BLK)
-        grad_self[:, span] = chunks[place, :width].astype(jnp.float32)
-        grad_neigh[:, span] = chunks[count + place, :width].astype(jnp.float32)
+    order = interleave()
+    for path, out in enumerate((grad_self, grad_neigh)):
+        for place in range(4):
+            pair = jnp.concatenate(
+                [chunks[8 * path + 4 * half + place, :width] for half in range(2)], axis=1
+            )
+            out[:, 2 * place * BLK : 2 * (place + 1) * BLK] = lax.dot_general(
+                pair, order, (((1,), (1,)), ((), ())), preferred_element_type=jnp.float32
+            )
 
 
 def whole(*shape):
@@ -248,7 +298,7 @@
     parts = lax.axis_size("dom")
     shards = lax.axis_size("feat")
     dims = width * shards
-    total = dims + 4 * BLK
+    outs = dims // 2
     send_blocks = jnp.transpose(send_blocks, (0, 2, 1))
     core = (lax.axis_index("feat") % 2).astype(jnp.int32).reshape(1)
     tiles = near(tile_values[0])
@@ -266,10 +316,10 @@
     bias = jnp.pad(pieces(out_bias), ((0, 0), (0, BLK - 3)))
     packed = pl.pallas_call(
         pack_kernel,
-        out_shape=HBM((shards, width, total), bf16),
+        out_shape=HBM((shards, HEIGHT, BLK), bf16),
         grid=(1,),
         in_specs=[whole(width, dims), whole(width, dims), whole(width, ROWS), whole(width, BLK)],
-        out_specs=part_of((shards, width, dims + 2 * BLK), 0, 0, 0),
+        out_specs=whole(shards, HEIGHT, BLK),
         compiler_params=PARAMS,
         name="pack",
     )(weight_self, weight_neigh, out_cotangent, bias)
@@ -277,7 +327,7 @@
     packed, divisor = pl.pallas_call(
         aggregate_kernel,
         out_shape=(
-            HBM((shards, width, total), bf16),
+            HBM((shards, HEIGHT, BLK), bf16),
             pltpu.VMEM((NBLK, BLK), f32),
         ),
         grid=(1,),
@@ -290,7 +340,7 @@
             VMEM,
             pl.BlockSpec(memory_space=pl.ANY),
         ],
-        out_specs=(part_of((shards, width, 2 * BLK), 0, 0, dims // (2 * BLK) + 1), VMEM),
+        out_specs=(part_of((shards, 4 * 32, BLK), 0, 1, 0), VMEM),
         scratch_shapes=[
             pltpu.VMEM((NBLK + parts * CAP, width + 16, BLK), bf16),
             pltpu.VMEM((NBLK + 1, width + 16, BLK), f32),
@@ -299,14 +349,18 @@
         compiler_params=PARAMS,
         name="aggregate",
     )(tile_rows, tile_cols, tile_count, near(node_feats), near(halo), tiles, packed)
-    packed = near(swap(packed, "feat").reshape(dims, total))
-
-    chunk = 2 * BLK
-    keep, send = pl.pallas_call(
+    packed = near(swap(packed, "feat"))
+
+    weight, data, keep, send = pl.pallas_call(
         pre_kernel,
-        out_shape=(pltpu.VMEM((dims, BLK), f32), jax.ShapeDtypeStruct((dims, BLK), f32)),
+        out_shape=(
+            pltpu.VMEM((dims, outs), bf16),
+            pltpu.VMEM((dims, 4 * BLK), bf16),
+            pltpu.VMEM((outs, 2 * BLK), f32),
+            jax.ShapeDtypeStruct((outs, 2 * BLK), f32),
+        ),
         in_specs=[SMEM, VMEM],
-        out_specs=(VMEM, VMEM),
+        out_specs=(VMEM,) * 4,
         compiler_params=PARAMS,
         name="pre",
     )(core, packed)
@@ -314,10 +368,10 @@
     layer, grad, local, sums = pl.pallas_call(
         slope_kernel,
         out_shape=(
-            pltpu.VMEM((dims, BLK), bf16),
-            jax.ShapeDtypeStruct((dims, BLK), bf16),
-            pltpu.VMEM((dims, BLK), bf16),
-            pltpu.VMEM((dims, BLK), bf16),
+            pltpu.VMEM((outs, 2 * BLK), bf16),
+            jax.ShapeDtypeStruct((outs, 2 * BLK), bf16),
+            pltpu.VMEM((outs, 2 * BLK), bf16),
+            pltpu.VMEM((outs, BLK), bf16),
         ),
         in_specs=[VMEM, VMEM, VMEM],
         out_specs=(VMEM,) * 4,
@@ -327,15 +381,15 @@
     other = lax.ppermute(grad, "feat", PAIRS)
     joined = pl.pallas_call(
         back_kernel,
-        out_shape=jax.ShapeDtypeStruct((dims, total), bf16),
-        grid=(dims // chunk,),
-        in_specs=[SMEM, VMEM, VMEM, VMEM, VMEM, VMEM],
-        out_specs=pl.BlockSpec((chunk, total), lambda i: (i, 0)),
-        scratch_shapes=[pltpu.VMEM((dims, chunk), bf16)],
+        out_shape=jax.ShapeDtypeStruct((shards, HEIGHT, BLK), bf16),
+        grid=(4,),
+        in_specs=[SMEM, VMEM, VMEM, VMEM, VMEM, VMEM, VMEM],
+        out_specs=pl.BlockSpec((shards // 4, HEIGHT, BLK), lambda i: (i, 0, 0)),
+        scratch_shapes=[pltpu.VMEM((outs, 4 * BLK), bf16)],
         compiler_params=PARAMS,
         name="back",
-    )(core, packed, near(local), near(other), near(layer), near(sums))
-    joined = swap(joined.reshape(shards, width, total), "feat")
+    )(core, near(weight), near(data), near(local), near(other), near(layer), near(sums))
+    joined = swap(joined, "feat")
 
     outgoing, own = pl.pallas_call(
         scatter_kernel,
@@ -354,8 +408,16 @@
     )(tile_rows, tile_cols, tile_count, near(joined), near(divisor), tiles)
     returned = near(swap(outgoing, "dom"))
 
-    layer_out = jnp.transpose(joined[:, :, dims : dims + BLK], (1, 0, 2)).reshape(width, ROWS)
-    bias_part = jnp.sum(joined[:, :, dims + BLK : dims + BLK + 3].astype(f32), axis=(0, 2))
+    layer_out = pl.pallas_call(
+        layer_kernel,
+        out_shape=jax.ShapeDtypeStruct((width, ROWS), bf16),
+        in_specs=[VMEM],
+        out_specs=VMEM,
+        compiler_params=PARAMS,
+        name="layer",
+    )(near(joined))
+    bias_part = joined[:, TAIL:, :3].astype(f32).reshape(shards // 4, 2, 2, 16, 3)
+    bias_part = jnp.sum(bias_part, axis=(0, 2, 4)).reshape(width)
     scale = 1.0 / float(ROWS * parts) ** 0.5
     extra = jnp.pad(pieces(bias_part * scale).T, ((0, 13), (0, BLK - width)))
     chunks = pl.pallas_call(

time: 203 us -> 187 us (0.921)
  blocking collectives: 43.2 us -> 35.6 us
  waiting for transfers between devices: 90.4 us -> 84 us
    all_to_all x1, blocking collectives: 43.2 us -> 35.6 us  [swap(): return lax.all_to_all(values, axis, split_axis=0, concat_axis=0, tiled=True)]
    all_to_all x4, waiting for transfers between devices: 87.2 us -> 80.7 us  [swap(): return lax.all_to_all(values, axis, split_axis=0, concat_axis=0, tiled=True)]
    pallas_call x5 -> x6, Pallas kernels: 7.79 us -> 8.84 us  [the longest x1 2.75 us: per_device(): pl.pallas_call(aggregate_kernel, out_shape=(HBM((shards, HEIGHT, BLK), bf...]
where the time goes in v4:
time: 187 us
  waiting for transfers between devices  84 us (45%)
  starting transfers between devices  43 us (23%)
  blocking collectives  35.6 us (19%)
  Pallas kernels  15.6 us (8%)
  local copies, waits for them, and re-layouts  5.81 us (3%)
    all_to_all x4, waiting for transfers between devices, swap(): return lax.all_to_all(values, axis, split_axis=0, concat_axis=0, tiled=True)  80.7 us
    all_to_all x4, starting transfers between devices, swap(): return lax.all_to_all(values, axis, split_axis=0, concat_axis=0, tiled=True)  39 us
    all_to_all x1, blocking collectives, swap(): return lax.all_to_all(values, axis, split_axis=0, concat_axis=0, tiled=True)  35.6 us
    unnamed x26, local copies, waits for them, and re-layouts  5.61 us
  transfers between devices with their start and end apart: 6, of which 6 were waited for; matrix products, arithmetic and copies ran while one was open for 1% of the time, Pallas kernels for 2%

profile of v4, /device:TPU:32, one launch (start us, length us, event | category | flops | bytes accessed | tf_op | source)
XLA Modules:
  0.0 186.8 jit_solution(15387484607531031692)
XLA Ops:
  0.7 1.1 copy-done.2
  1.7 0.7 copy-done.9
  2.4 1.3 outgoing.1
  3.7 15.2 %all-to-all-start = ((bf16[16,32,256]{2,1,0:T(8,128)(2,1)}), bf16[16,32,256]{2,1,0:T(8,128)(2,1)S(1)}, u32[]{:S(2)}, u32[]{:S(2)}) async-start(bf16[16,32,256]{2,1,0:T(8,128)(2,1)} %outgoing.1), calls=%async_computation | async-start | bytes 524288 | tf_op jit(solution)/shard_map/all_to_all | solution.py:281
  19.6 0.7 fusion
  20.4 0.9 copy-done.6
  21.4 0.8 copy-done.7
  22.2 0.8 copy-done.8
  23.0 1.8 pack.1.packed
  24.9 12.0 %all-to-all-done.halo = bf16[16,32,256]{2,1,0:T(8,128)(2,1)S(1)} async-done(((bf16[16,32,256]{2,1,0:T(8,128)(2,1)}), bf16[16,32,256]{2,1,0:T(8,128)(2,1)S(1)}, u32[]{:S(2)}, u32[]{:S(2)}) %all-to-all-start) | async-done | bytes 262176 | tf_op jit(solution)/shard_map/all_to_all | solution.py:281
  36.9 2.8 %aggregate.1 = (bf16[32,304,128]{2,1,0:T(8,128)(2,1)}, f32[32,128]{1,0:T(8,128)S(1)}) custom-call(s32[1,64]{1,0:T(1,128)S(1)} %copy-done.11, s32[1,64]{1,0:T(1,128)S(1)} %copy-done.12, s32[1]{0:T(128)S(6)} %copy.25.count, bf16[32,4096]{1,0:T(8,128)(2,1)S(1)} %copy-done.3, ...), custom_call_target="tpu_custom_call", output_to_operand_aliasing={{0}: (6, {})} | custom-call | tf_op jit(solution)/shard_map/aggregate/pallas_call | solution.py:327
  39.6 7.3 %all-to-all-start.1 = ((bf16[32,304,128]{2,1,0:T(8,128)(2,1)}), bf16[32,304,128]{2,1,0:T(8,128)(2,1)S(1)}, u32[]{:S(2)}, u32[]{:S(2)}) async-start(bf16[32,304,128]{2,1,0:T(8,128)(2,1)} %get-tuple-element.19), calls=%async_computation.1 | async-start | bytes 4980736 | tf_op jit(solution)/shard_map/all_to_all | solution.py:281
  47.0 33.2 %all-to-all-done.1.packed = bf16[32,304,128]{2,1,0:T(8,128)(2,1)S(1)} async-done(((bf16[32,304,128]{2,1,0:T(8,128)(2,1)}), bf16[32,304,128]{2,1,0:T(8,128)(2,1)S(1)}, u32[]{:S(2)}, u32[]{:S(2)}) %all-to-all-start.1) | async-done | bytes 2490400 | tf_op jit(solution)/shard_map/all_to_all | solution.py:281
  80.1 0.9 pre.1
  81.1 1.9 %collective-permute-start = (f32[512,256]{1,0:T(8,128)S(1)}, f32[512,256]{1,0:T(8,128)S(1)}, u32[]{:S(2)}, u32[]{:S(2)}) collective-permute-start(f32[512,256]{1,0:T(8,128)S(1)} %get-tuple-element.23), channel_id=1, source_target_pairs={{0,1},{1,0},{2,3},{3,2},{4,5},{5,4},{6,7},{7,6},{8,9},{9,8},{10,11... | collective-permute-start | bytes 1572872 | tf_op jit(solution)/shard_map/ppermute | solution.py:367
  83.0 1.9 %collective-permute-done.received = f32[512,256]{1,0:T(8,128)S(1)} collective-permute-done((f32[512,256]{1,0:T(8,128)S(1)}, f32[512,256]{1,0:T(8,128)S(1)}, u32[]{:S(2)}, u32[]{:S(2)}) %collective-permute-start) | collective-permute-done | bytes 524320 | tf_op jit(solution)/shard_map/ppermute | solution.py:367
  84.9 0.6 slope.1
  85.5 2.0 %collective-permute-start.1 = (bf16[512,256]{1,0:T(8,128)(2,1)S(1)}, bf16[512,256]{1,0:T(8,128)(2,1)S(1)}, u32[]{:S(2)}, u32[]{:S(2)}) collective-permute-start(bf16[512,256]{1,0:T(8,128)(2,1)S(1)} %get-tuple-element.25), channel_id=1, source_target_pairs={{0,1},{1,0},{2,3},{3,2},{4,5},{5,4},{6,7},{7,6},{8,9},{9,8},{10,11... | collective-permute-start | bytes 786440 | tf_op jit(solution)/shard_map/ppermute | solution.py:381
  87.6 1.4 collective-permute-done.1.other
  88.9 2.0 %back.1 = bf16[32,304,128]{2,1,0:T(8,128)(2,1)S(1)} custom-call(s32[1]{0:T(128)} %bitcast.core, bf16[1024,512]{1,0:T(8,128)(2,1)S(1)} %get-tuple-element.20.weight, bf16[1024,512]{1,0:T(8,128)(2,1)S(1)} %get-tuple-element.21.data, bf16[512,256]{1,0:T(8,128)(2,1)S(1)} %get-tuple-element.24.grad, bf16[512,256]{1,0:T(8,128)(2,1)S(1)} %collective-permute-done.1.other, ...), custom_call_target="tpu_custom_call" | custom-call | tf_op jit(solution)/shard_map/back/pallas_call | solution.py:382
  90.9 35.6 %all_to_all.25.joined = bf16[32,304,128]{2,1,0:T(8,128)(2,1)S(1)} all-to-all(bf16[32,304,128]{2,1,0:T(8,128)(2,1)S(1)} %back.1), channel_id=1, replica_groups=mesh['dom'=16,'feat'=32] {'feat'}, dimensions={0} | all-to-all | bytes 4980736 | tf_op jit(solution)/shard_map/all_to_all | solution.py:281
  126.5 2.2 %scatter.1 = (bf16[16,32,384]{2,1,0:T(8,128)(2,1)}, f32[32,4096]{1,0:T(8,128)S(1)}) custom-call(s32[1,64]{1,0:T(1,128)S(1)} %copy-done.11, s32[1,64]{1,0:T(1,128)S(1)} %copy-done.12, s32[1]{0:T(128)S(6)} %copy.25.count, bf16[32,304,128]{2,1,0:T(8,128)(2,1)S(1)} %all_to_all.25.joined, f32[32,128]{1,0:T(8,128)S(1)} %get-tuple-element.28.divisor, ...), custom_call_target="tpu_custom_call" | custom-call | tf_op jit(solution)/shard_map/scatter/pallas_call | solution.py:394
  128.7 0.8 copy-done.4
  129.5 8.3 %all-to-all-start.3 = ((bf16[16,32,384]{2,1,0:T(8,128)(2,1)}), bf16[16,32,384]{2,1,0:T(8,128)(2,1)S(1)}, u32[]{:S(2)}, u32[]{:S(2)}) async-start(bf16[16,32,384]{2,1,0:T(8,128)(2,1)} %get-tuple-element.30), calls=%async_computation.3 | async-start | bytes 786432 | tf_op jit(solution)/shard_map/all_to_all | solution.py:281
  138.2 22.1 %all-to-all-done.3.returned.terms = bf16[16,32,384]{2,1,0:T(8,128)(2,1)S(1)} async-done(((bf16[16,32,384]{2,1,0:T(8,128)(2,1)}), bf16[16,32,384]{2,1,0:T(8,128)(2,1)S(1)}, u32[]{:S(2)}, u32[]{:S(2)}) %all-to-all-start.3) | async-done | bytes 393248 | tf_op jit(solution)/shard_map/all_to_all | solution.py:281
  160.2 0.7 piece.1
  160.9 8.2 %all-to-all-start.4 = ((bf16[16,48,128]{2,1,0:T(8,128)(2,1)}), bf16[16,48,128]{2,1,0:T(8,128)(2,1)S(1)}, u32[]{:S(2)}, u32[]{:S(2)}) async-start(bf16[16,48,128]{2,1,0:T(8,128)(2,1)} %piece.1), calls=%async_computation.4 | async-start | bytes 393216 | tf_op jit(solution)/shard_map/all_to_all | solution.py:281
  169.1 0.7 layer.1
  170.2 1.5 collect.1
  171.7 13.5 %all-to-all-done.4.chunks = bf16[16,48,128]{2,1,0:T(8,128)(2,1)S(1)} async-done(((bf16[16,48,128]{2,1,0:T(8,128)(2,1)}), bf16[16,48,128]{2,1,0:T(8,128)(2,1)S(1)}, u32[]{:S(2)}, u32[]{:S(2)}) %all-to-all-start.4) | async-done | bytes 196640 | tf_op jit(solution)/shard_map/all_to_all | solution.py:281
  185.2 0.5 convert_reduce_fusion.1
  185.7 1.1 finish.1
  (30 shorter events, 0.8 us)
Async XLA Ops:
  0.6 36.2 %copy-start = (bf16[1,64,128,128]{3,2,1,0:T(8,128)(2,1)S(1)}, bf16[1,64,128,128]{3,2,1,0:T(8,128)(2,1)}, u32[]{:S(2)}) copy-start(bf16[1,64,128,128]{3,2,1,0:T(8,128)(2,1)} %param.19) | copy-start | bytes 6291460
  0.6 1.1 copy-start.2
  1.7 0.7 copy-start.9
  2.4 34.5 %copy-start.3 = (bf16[32,4096]{1,0:T(8,128)(2,1)S(1)}, bf16[32,4096]{1,0:T(8,128)(2,1)}, u32[]{:S(2)}) copy-start(bf16[32,4096]{1,0:T(8,128)(2,1)} %feats.3) | copy-start | bytes 786436
  3.7 33.1 %all-to-all-start = ((bf16[16,32,256]{2,1,0:T(8,128)(2,1)}), bf16[16,32,256]{2,1,0:T(8,128)(2,1)S(1)}, u32[]{:S(2)}, u32[]{:S(2)}) async-start(bf16[16,32,256]{2,1,0:T(8,128)(2,1)} %outgoing.1), calls=%async_computation | async-start | bytes 524288 | tf_op jit(solution)/shard_map/all_to_all | solution.py:281
  20.4 1.0 copy-start.6
  21.4 0.8 copy-start.7
  22.2 0.8 copy-start.8
  23.0 13.8 %copy-start.11 = (s32[1,64]{1,0:T(1,128)S(1)}, s32[1,64]{1,0:T(1,128)}, u32[]{:S(2)}) copy-start(s32[1,64]{1,0:T(1,128)} %rows.3) | copy-start | bytes 772
  23.0 13.8 %copy-start.12 = (s32[1,64]{1,0:T(1,128)S(1)}, s32[1,64]{1,0:T(1,128)}, u32[]{:S(2)}) copy-start(s32[1,64]{1,0:T(1,128)} %cols.3) | copy-start | bytes 772
  39.6 40.5 %all-to-all-start.1 = ((bf16[32,304,128]{2,1,0:T(8,128)(2,1)}), bf16[32,304,128]{2,1,0:T(8,128)(2,1)S(1)}, u32[]{:S(2)}, u32[]{:S(2)}) async-start(bf16[32,304,128]{2,1,0:T(8,128)(2,1)} %get-tuple-element.19), calls=%async_computation.1 | async-start | bytes 4980736 | tf_op jit(solution)/shard_map/all_to_all | solution.py:281
  81.1 3.8 %collective-permute-start = (f32[512,256]{1,0:T(8,128)S(1)}, f32[512,256]{1,0:T(8,128)S(1)}, u32[]{:S(2)}, u32[]{:S(2)}) collective-permute-start(f32[512,256]{1,0:T(8,128)S(1)} %get-tuple-element.23), channel_id=1, source_target_pairs={{0,1},{1,0},{2,3},{3,2},{4,5},{5,4},{6,7},{7,6},{8,9},{9,8},{10,11... | collective-permute-start | bytes 1572872 | tf_op jit(solution)/shard_map/ppermute | solution.py:367
  85.5 3.4 %collective-permute-start.1 = (bf16[512,256]{1,0:T(8,128)(2,1)S(1)}, bf16[512,256]{1,0:T(8,128)(2,1)S(1)}, u32[]{:S(2)}, u32[]{:S(2)}) collective-permute-start(bf16[512,256]{1,0:T(8,128)(2,1)S(1)} %get-tuple-element.25), channel_id=1, source_target_pairs={{0,1},{1,0},{2,3},{3,2},{4,5},{5,4},{6,7},{7,6},{8,9},{9,8},{10,11... | collective-permute-start | bytes 786440 | tf_op jit(solution)/shard_map/ppermute | solution.py:381
  90.9 35.6 %copy-start.1 = (bf16[1,64,128,128]{3,2,1,0:T(8,128)(2,1)S(1)}, bf16[1,64,128,128]{3,2,1,0:T(8,128)(2,1)}, u32[]{:S(2)}) copy-start(bf16[1,64,128,128]{3,2,1,0:T(8,128)(2,1)} %param.19) | copy-start | bytes 6291460
  128.7 0.8 copy-start.4
  129.5 40.3 %copy-start.10 = (s32[1,16,2]{1,2,0:T(2,128)S(1)}, s32[1,16,2]{1,2,0:T(2,128)}, u32[]{:S(2)}) copy-start(s32[1,16,2]{1,2,0:T(2,128)} %param.15) | copy-start | bytes 388
  129.5 30.7 %all-to-all-start.3 = ((bf16[16,32,384]{2,1,0:T(8,128)(2,1)}), bf16[16,32,384]{2,1,0:T(8,128)(2,1)S(1)}, u32[]{:S(2)}, u32[]{:S(2)}) async-start(bf16[16,32,384]{2,1,0:T(8,128)(2,1)} %get-tuple-element.30), calls=%async_computation.3 | async-start | bytes 786432 | tf_op jit(solution)/shard_map/all_to_all | solution.py:281
  160.9 24.3 %all-to-all-start.4 = ((bf16[16,48,128]{2,1,0:T(8,128)(2,1)}), bf16[16,48,128]{2,1,0:T(8,128)(2,1)S(1)}, u32[]{:S(2)}, u32[]{:S(2)}) async-start(bf16[16,48,128]{2,1,0:T(8,128)(2,1)} %piece.1), calls=%async_computation.4 | async-start | bytes 393216 | tf_op jit(solution)/shard_map/all_to_all | solution.py:281
  169.1 1.1 copy-start.5

commit v5 on v4

--- a/solution.py
+++ b/solution.py
@@ -25,10 +25,21 @@
     return pl.ds(pl.multiple_of(block * BLK, BLK), BLK)
 
 
-def outgoing_kernel(sends, feats, out):
+def outgoing_kernel(sends, feats, out, sems):
+    copies = []
     for part in range(out.shape[0]):
         for place in range(CAP):
-            out[part, :, place * BLK : (place + 1) * BLK] = feats[:, lanes(sends[0, place, part])]
+            copies.append(
+                pltpu.make_async_copy(
+                    feats.at[:, lanes(sends[0, place, part])],
+                    out.at[part, :, place * BLK : (place + 1) * BLK],
+                    sems.at[part, place],
+                )
+            )
+    for copy in copies:
+        copy.start()
+    for copy in copies:
+        copy.wait()
 
 
 SIDE = 8 * 32
@@ -236,7 +247,7 @@
     out[...] = acc[...].astype(jnp.bfloat16)
 
 
-def finish_kernel(chunks, grad_self, grad_neigh):
+def finish_kernel(chunks, grad_self, grad_neigh, grad_bias):
     width = grad_self.shape[0]
     order = interleave()
     for path, out in enumerate((grad_self, grad_neigh)):
@@ -247,6 +258,10 @@
             out[:, 2 * place * BLK : 2 * (place + 1) * BLK] = lax.dot_general(
                 pair, order, (((1,), (1,)), ((), ())), preferred_element_type=jnp.float32
             )
+    total = chunks[0, width:].astype(jnp.float32)
+    for part in range(1, chunks.shape[0]):
+        total += chunks[part, width:].astype(jnp.float32)
+    grad_bias[...] = jnp.sum(total, axis=0, keepdims=True)
 
 
 def whole(*shape):
@@ -255,6 +270,10 @@
 
 def near(array):
     return pltpu.with_memory_space_constraint(array, pltpu.MemorySpace.VMEM)
+
+
+def far(array):
+    return pltpu.with_memory_space_constraint(array, HBM)
 
 
 def part_of(shape, *index):
@@ -305,12 +324,13 @@
 
     outgoing = pl.pallas_call(
         outgoing_kernel,
-        out_shape=jax.ShapeDtypeStruct((parts, width, CAP * BLK), bf16),
-        in_specs=[SMEM, VMEM],
-        out_specs=VMEM,
+        out_shape=HBM((parts, width, CAP * BLK), bf16),
+        in_specs=[SMEM, pl.BlockSpec(memory_space=HBM)],
+        out_specs=pl.BlockSpec(memory_space=HBM),
+        scratch_shapes=[pltpu.SemaphoreType.DMA((parts, CAP))],
         compiler_params=PARAMS,
         name="outgoing",
-    )(send_blocks, node_feats)
+    )(far(send_blocks), far(node_feats))
     halo = swap(outgoing, "dom")
 
     bias = jnp.pad(pieces(out_bias), ((0, 0), (0, BLK - 3)))
@@ -395,7 +415,7 @@
         scatter_kernel,
         out_shape=(
             HBM((parts, width, (CAP + 1) * BLK), bf16),
-            pltpu.VMEM((width, ROWS), f32),
+            HBM((width, ROWS), f32),
         ),
         in_specs=[SMEM, SMEM, SMEM, VMEM, VMEM, VMEM],
         out_specs=(VMEM, VMEM),
@@ -419,10 +439,10 @@
     bias_part = joined[:, TAIL:, :3].astype(f32).reshape(shards // 4, 2, 2, 16, 3)
     bias_part = jnp.sum(bias_part, axis=(0, 2, 4)).reshape(width)
     scale = 1.0 / float(ROWS * parts) ** 0.5
-    extra = jnp.pad(pieces(bias_part * scale).T, ((0, 13), (0, BLK - width)))
+    extra = jnp.pad(pieces(bias_part * scale).T, ((0, 5), (0, BLK - width)))
     chunks = pl.pallas_call(
         functools.partial(piece_kernel, scale=scale),
-        out_shape=HBM((parts, width + 16, BLK), bf16),
+        out_shape=HBM((parts, width + 8, BLK), bf16),
         in_specs=[VMEM, VMEM],
         out_specs=VMEM,
         compiler_params=PARAMS,
@@ -438,15 +458,16 @@
         compiler_params=PARAMS,
         name="collect",
     )(send_blocks, near(own), returned)
-    grad_self, grad_neigh = pl.pallas_call(
+    grad_self, grad_neigh, grad_bias = pl.pallas_call(
         finish_kernel,
-        out_shape=(jax.ShapeDtypeStruct((width, dims), f32),) * 2,
+        out_shape=(jax.ShapeDtypeStruct((width, dims), f32),) * 2
+        + (jax.ShapeDtypeStruct((1, BLK), f32),),
         in_specs=[VMEM],
-        out_specs=(VMEM, VMEM),
+        out_specs=(VMEM,) * 3,
         compiler_params=PARAMS,
         name="finish",
     )(near(chunks))
-    grad_bias = jnp.sum(chunks[:, width : width + 3, :width].astype(f32), axis=(0, 1))
+    grad_bias = grad_bias[0, :width]
     return (layer_out, feats_grad, grad_self, grad_neigh, grad_bias)
 
 

time: 187 us -> 192 us (1.027)
  Pallas kernels: 15.6 us -> 24.5 us
  local copies, waits for them, and re-layouts: 5.81 us -> 3.75 us
    pallas_call x1, Pallas kernels: 1.32 us -> 10.2 us  [per_device(): pl.pallas_call(outgoing_kernel, out_shape=HBM((parts, width, CAP * BLK),...]
    unnamed x26 -> x20, local copies, waits for them, and re-layouts: 5.61 us -> 3.03 us
where the time goes in v5:
time: 192 us
  waiting for transfers between devices  82.9 us (43%)
  starting transfers between devices  42.7 us (22%)
  blocking collectives  35.6 us (19%)
  Pallas kernels  24.5 us (13%)
  local copies, waits for them, and re-layouts  3.75 us (2%)
    all_to_all x4, waiting for transfers between devices, swap(): return lax.all_to_all(values, axis, split_axis=0, concat_axis=0, tiled=True)  79.6 us
    all_to_all x4, starting transfers between devices, swap(): return lax.all_to_all(values, axis, split_axis=0, concat_axis=0, tiled=True)  38.7 us
    all_to_all x1, blocking collectives, swap(): return lax.all_to_all(values, axis, split_axis=0, concat_axis=0, tiled=True)  35.6 us
    pallas_call x1, Pallas kernels, per_device(): pl.pallas_call(outgoing_kernel, out_shape=HBM((parts, width, CAP * BLK),...  10.2 us
  transfers between devices with their start and end apart: 6, of which 6 were waited for; matrix products, arithmetic and copies ran while one was open for 1% of the time, Pallas kernels for 2%

profile of v5, /device:TPU:32, one launch (start us, length us, event | category | flops | bytes accessed | tf_op | source)
XLA Modules:
  0.0 191.7 jit_solution(3196977141488882822)
XLA Ops:
  0.7 10.2 %outgoing.1 = bf16[16,32,256]{2,1,0:T(8,128)(2,1)} custom-call(s32[1,2,16]{2,1,0:T(2,128)} %bitcast.16, bf16[32,4096]{1,0:T(8,128)(2,1)} %feats.3), custom_call_target="tpu_custom_call" | custom-call | tf_op jit(solution)/shard_map/outgoing/pallas_call | solution.py:325
  10.8 15.2 %all-to-all-start = ((bf16[16,32,256]{2,1,0:T(8,128)(2,1)}), bf16[16,32,256]{2,1,0:T(8,128)(2,1)S(1)}, u32[]{:S(2)}, u32[]{:S(2)}) async-start(bf16[16,32,256]{2,1,0:T(8,128)(2,1)} %outgoing.1), calls=%async_computation | async-start | bytes 524288 | tf_op jit(solution)/shard_map/all_to_all | solution.py:300
  26.7 0.7 fusion
  27.4 0.1 copy.21
  27.5 0.9 copy-done.4
  28.5 0.8 copy-done.5
  29.3 0.8 copy-done.6
  30.1 1.8 pack.1.packed
  32.0 12.0 %all-to-all-done.halo = bf16[16,32,256]{2,1,0:T(8,128)(2,1)S(1)} async-done(((bf16[16,32,256]{2,1,0:T(8,128)(2,1)}), bf16[16,32,256]{2,1,0:T(8,128)(2,1)S(1)}, u32[]{:S(2)}, u32[]{:S(2)}) %all-to-all-start) | async-done | bytes 262176 | tf_op jit(solution)/shard_map/all_to_all | solution.py:300
  44.0 2.7 %aggregate.1 = (bf16[32,304,128]{2,1,0:T(8,128)(2,1)}, f32[32,128]{1,0:T(8,128)S(1)}) custom-call(s32[1,64]{1,0:T(1,128)S(1)} %copy-done.8, s32[1,64]{1,0:T(1,128)S(1)} %copy-done.9, s32[1]{0:T(128)S(6)} %copy.25.count, bf16[32,4096]{1,0:T(8,128)(2,1)S(1)} %copy-done.2, bf16[16,32,256]{2,1,0:T(8,128)(2,1)S(1)} %all-to-all-done.halo, ...), custom_call_target="tpu_custom_call", output_to_operand_aliasing={{0}: (6, {})} | custom-call | tf_op jit(solution)/shard_map/aggregate/pallas_call | solution.py:347
  46.7 7.3 %all-to-all-start.1 = ((bf16[32,304,128]{2,1,0:T(8,128)(2,1)}), bf16[32,304,128]{2,1,0:T(8,128)(2,1)S(1)}, u32[]{:S(2)}, u32[]{:S(2)}) async-start(bf16[32,304,128]{2,1,0:T(8,128)(2,1)} %get-tuple-element.20), calls=%async_computation.1 | async-start | bytes 4980736 | tf_op jit(solution)/shard_map/all_to_all | solution.py:300
  54.1 33.2 %all-to-all-done.1.packed = bf16[32,304,128]{2,1,0:T(8,128)(2,1)S(1)} async-done(((bf16[32,304,128]{2,1,0:T(8,128)(2,1)}), bf16[32,304,128]{2,1,0:T(8,128)(2,1)S(1)}, u32[]{:S(2)}, u32[]{:S(2)}) %all-to-all-start.1) | async-done | bytes 2490400 | tf_op jit(solution)/shard_map/all_to_all | solution.py:300
  87.2 0.9 pre.1
  88.2 1.9 %collective-permute-start = (f32[512,256]{1,0:T(8,128)S(1)}, f32[512,256]{1,0:T(8,128)S(1)}, u32[]{:S(2)}, u32[]{:S(2)}) collective-permute-start(f32[512,256]{1,0:T(8,128)S(1)} %get-tuple-element.24), channel_id=1, source_target_pairs={{0,1},{1,0},{2,3},{3,2},{4,5},{5,4},{6,7},{7,6},{8,9},{9,8},{10,11... | collective-permute-start | bytes 1572872 | tf_op jit(solution)/shard_map/ppermute | solution.py:387
  90.1 1.9 collective-permute-done.received
  92.0 0.6 slope.1
  92.6 2.0 %collective-permute-start.1 = (bf16[512,256]{1,0:T(8,128)(2,1)S(1)}, bf16[512,256]{1,0:T(8,128)(2,1)S(1)}, u32[]{:S(2)}, u32[]{:S(2)}) collective-permute-start(bf16[512,256]{1,0:T(8,128)(2,1)S(1)} %get-tuple-element.26), channel_id=1, source_target_pairs={{0,1},{1,0},{2,3},{3,2},{4,5},{5,4},{6,7},{7,6},{8,9},{9,8},{10,11... | collective-permute-start | bytes 786440 | tf_op jit(solution)/shard_map/ppermute | solution.py:401
  94.7 1.4 collective-permute-done.1.other
  96.0 2.0 %back.1 = bf16[32,304,128]{2,1,0:T(8,128)(2,1)S(1)} custom-call(s32[1]{0:T(128)} %bitcast.core, bf16[1024,512]{1,0:T(8,128)(2,1)S(1)} %get-tuple-element.21.weight, bf16[1024,512]{1,0:T(8,128)(2,1)S(1)} %get-tuple-element.22.data, bf16[512,256]{1,0:T(8,128)(2,1)S(1)} %get-tuple-element.25.grad, bf16[512,256]{1,0:T(8,128)(2,1)S(1)} %collective-permute-done.1.other, ...), custom_call_target="tpu_custom_call" | custom-call | tf_op jit(solution)/shard_map/back/pallas_call | solution.py:402
  98.0 35.6 %all_to_all.25.joined = bf16[32,304,128]{2,1,0:T(8,128)(2,1)S(1)} all-to-all(bf16[32,304,128]{2,1,0:T(8,128)(2,1)S(1)} %back.1), channel_id=1, replica_groups=mesh['dom'=16,'feat'=32] {'feat'}, dimensions={0} | all-to-all | bytes 4980736 | tf_op jit(solution)/shard_map/all_to_all | solution.py:300
  133.6 2.2 %scatter.1 = (bf16[16,32,384]{2,1,0:T(8,128)(2,1)}, f32[32,4096]{1,0:T(8,128)}) custom-call(s32[1,64]{1,0:T(1,128)S(1)} %copy-done.8, s32[1,64]{1,0:T(1,128)S(1)} %copy-done.9, s32[1]{0:T(128)S(6)} %copy.25.count, bf16[32,304,128]{2,1,0:T(8,128)(2,1)S(1)} %all_to_all.25.joined, f32[32,128]{1,0:T(8,128)S(1)} %get-tuple-element.29.divisor, ...), custom_call_target="tpu_custom_call" | custom-call | tf_op jit(solution)/shard_map/scatter/pallas_call | solution.py:414
  135.9 8.0 %all-to-all-start.3 = ((bf16[16,32,384]{2,1,0:T(8,128)(2,1)}), bf16[16,32,384]{2,1,0:T(8,128)(2,1)S(1)}, u32[]{:S(2)}, u32[]{:S(2)}) async-start(bf16[16,32,384]{2,1,0:T(8,128)(2,1)} %get-tuple-element.31), calls=%async_computation.3 | async-start | bytes 786432 | tf_op jit(solution)/shard_map/all_to_all | solution.py:300
  143.8 0.1 convert_reduce_fusion
  144.1 22.1 %all-to-all-done.3.returned.terms = bf16[16,32,384]{2,1,0:T(8,128)(2,1)S(1)} async-done(((bf16[16,32,384]{2,1,0:T(8,128)(2,1)}), bf16[16,32,384]{2,1,0:T(8,128)(2,1)S(1)}, u32[]{:S(2)}, u32[]{:S(2)}) %all-to-all-start.3) | async-done | bytes 393248 | tf_op jit(solution)/shard_map/all_to_all | solution.py:300
  166.2 0.7 piece.1
  166.9 8.2 %all-to-all-start.4 = ((bf16[16,40,128]{2,1,0:T(8,128)(2,1)}), bf16[16,40,128]{2,1,0:T(8,128)(2,1)S(1)}, u32[]{:S(2)}, u32[]{:S(2)}) async-start(bf16[16,40,128]{2,1,0:T(8,128)(2,1)} %piece.1), calls=%async_computation.4 | async-start | bytes 327680 | tf_op jit(solution)/shard_map/all_to_all | solution.py:300
  175.1 0.7 layer.1
  175.8 0.4 copy-done.3
  176.2 1.5 collect.1
  177.7 12.4 %all-to-all-done.4.chunks = bf16[16,40,128]{2,1,0:T(8,128)(2,1)S(1)} async-done(((bf16[16,40,128]{2,1,0:T(8,128)(2,1)}), bf16[16,40,128]{2,1,0:T(8,128)(2,1)S(1)}, u32[]{:S(2)}, u32[]{:S(2)}) %all-to-all-start.4) | async-done | bytes 163872 | tf_op jit(solution)/shard_map/all_to_all | solution.py:300
  190.1 1.1 finish.1
  191.2 0.5 slice_bitcast_fusion
  (24 shorter events, 0.2 us)
Async XLA Ops:
  0.6 43.3 %copy-start.2 = (bf16[32,4096]{1,0:T(8,128)(2,1)S(1)}, bf16[32,4096]{1,0:T(8,128)(2,1)}, u32[]{:S(2)}) copy-start(bf16[32,4096]{1,0:T(8,128)(2,1)} %feats.3) | copy-start | bytes 786436
  0.6 43.3 %copy-start = (bf16[1,64,128,128]{3,2,1,0:T(8,128)(2,1)S(1)}, bf16[1,64,128,128]{3,2,1,0:T(8,128)(2,1)}, u32[]{:S(2)}) copy-start(bf16[1,64,128,128]{3,2,1,0:T(8,128)(2,1)} %param.19) | copy-start | bytes 6291460
  10.8 33.1 %all-to-all-start = ((bf16[16,32,256]{2,1,0:T(8,128)(2,1)}), bf16[16,32,256]{2,1,0:T(8,128)(2,1)S(1)}, u32[]{:S(2)}, u32[]{:S(2)}) async-start(bf16[16,32,256]{2,1,0:T(8,128)(2,1)} %outgoing.1), calls=%async_computation | async-start | bytes 524288 | tf_op jit(solution)/shard_map/all_to_all | solution.py:300
  27.5 1.0 copy-start.4
  28.5 0.8 copy-start.5
  29.3 0.8 copy-start.6
  30.1 13.8 %copy-start.8 = (s32[1,64]{1,0:T(1,128)S(1)}, s32[1,64]{1,0:T(1,128)}, u32[]{:S(2)}) copy-start(s32[1,64]{1,0:T(1,128)} %rows.3) | copy-start | bytes 772
  30.1 13.8 %copy-start.9 = (s32[1,64]{1,0:T(1,128)S(1)}, s32[1,64]{1,0:T(1,128)}, u32[]{:S(2)}) copy-start(s32[1,64]{1,0:T(1,128)} %cols.3) | copy-start | bytes 772
  46.7 40.5 %all-to-all-start.1 = ((bf16[32,304,128]{2,1,0:T(8,128)(2,1)}), bf16[32,304,128]{2,1,0:T(8,128)(2,1)S(1)}, u32[]{:S(2)}, u32[]{:S(2)}) async-start(bf16[32,304,128]{2,1,0:T(8,128)(2,1)} %get-tuple-element.20), calls=%async_computation.1 | async-start | bytes 4980736 | tf_op jit(solution)/shard_map/all_to_all | solution.py:300
  88.2 3.8 %collective-permute-start = (f32[512,256]{1,0:T(8,128)S(1)}, f32[512,256]{1,0:T(8,128)S(1)}, u32[]{:S(2)}, u32[]{:S(2)}) collective-permute-start(f32[512,256]{1,0:T(8,128)S(1)} %get-tuple-element.24), channel_id=1, source_target_pairs={{0,1},{1,0},{2,3},{3,2},{4,5},{5,4},{6,7},{7,6},{8,9},{9,8},{10,11... | collective-permute-start | bytes 1572872 | tf_op jit(solution)/shard_map/ppermute | solution.py:387
  92.6 3.4 %collective-permute-start.1 = (bf16[512,256]{1,0:T(8,128)(2,1)S(1)}, bf16[512,256]{1,0:T(8,128)(2,1)S(1)}, u32[]{:S(2)}, u32[]{:S(2)}) collective-permute-start(bf16[512,256]{1,0:T(8,128)(2,1)S(1)} %get-tuple-element.26), channel_id=1, source_target_pairs={{0,1},{1,0},{2,3},{3,2},{4,5},{5,4},{6,7},{7,6},{8,9},{9,8},{10,11... | collective-permute-start | bytes 786440 | tf_op jit(solution)/shard_map/ppermute | solution.py:401
  98.0 35.6 %copy-start.1 = (bf16[1,64,128,128]{3,2,1,0:T(8,128)(2,1)S(1)}, bf16[1,64,128,128]{3,2,1,0:T(8,128)(2,1)}, u32[]{:S(2)}) copy-start(bf16[1,64,128,128]{3,2,1,0:T(8,128)(2,1)} %param.19) | copy-start | bytes 6291460
  135.9 40.0 %copy-start.7 = (s32[1,16,2]{1,2,0:T(2,128)S(1)}, s32[1,16,2]{1,2,0:T(2,128)}, u32[]{:S(2)}) copy-start(s32[1,16,2]{1,2,0:T(2,128)} %param.15) | copy-start | bytes 388
  135.9 30.3 %all-to-all-start.3 = ((bf16[16,32,384]{2,1,0:T(8,128)(2,1)}), bf16[16,32,384]{2,1,0:T(8,128)(2,1)S(1)}, u32[]{:S(2)}, u32[]{:S(2)}) async-start(bf16[16,32,384]{2,1,0:T(8,128)(2,1)} %get-tuple-element.31), calls=%async_computation.3 | async-start | bytes 786432 | tf_op jit(solution)/shard_map/all_to_all | solution.py:300
  166.9 23.2 %all-to-all-start.4 = ((bf16[16,40,128]{2,1,0:T(8,128)(2,1)}), bf16[16,40,128]{2,1,0:T(8,128)(2,1)S(1)}, u32[]{:S(2)}, u32[]{:S(2)}) async-start(bf16[16,40,128]{2,1,0:T(8,128)(2,1)} %piece.1), calls=%async_computation.4 | async-start | bytes 327680 | tf_op jit(solution)/shard_map/all_to_all | solution.py:300
  175.1 1.1 copy-start.3
